TPU v7x, 32 devices: a whole 2x2x4 slice. The times are simulated.
32 devices in a mesh: zone: 4 (over y, x), dev: 8 (over z, core).
Axes of the slice: x: 2, y: 2, z: 4, core: 2. Of those that a mesh axis runs over, the one named last changes fastest.
Arguments:
- node_features: bfloat16 [16384, 512], P(('zone', 'dev')), may hold values from -9 to 9
- neighbour_blocks: int32 [128, 32], P(('zone', 'dev')), may hold values from 0 to 127, as said below
- neighbour_count: int32 [128], P(('zone', 'dev')), may hold values from 8 to 32, as said below
- tile_valid: int32 [128], replicated, may hold values from 64 to 128
- w_query: bfloat16 [512, 512], replicated, may hold values from -0.5 to 0.5
- w_key: bfloat16 [512, 512], replicated, may hold values from -0.5 to 0.5
- w_value: bfloat16 [512, 512], replicated, may hold values from -0.25 to 0.25
- w_out: bfloat16 [512, 512], replicated, may hold values from -0.25 to 0.25
- w_gate: bfloat16 [512, 2048], replicated, may hold values from -0.25 to 0.25
- w_up: bfloat16 [512, 2048], replicated, may hold values from -0.25 to 0.25
- w_down: bfloat16 [2048, 512], replicated, may hold values from -0.125 to 0.125
Outputs:
- layer_out: bfloat16 [16384, 512], P(('zone', 'dev'))
Inputs may be any that keep to these rules, and one draw needn't show every extreme that they name: `neighbour_blocks`: each row lists 32 different blocks. Zones are runs of 32 blocks (zone of block g is g // 32); every listed block lies in the query block's zone or in one of the two zones beside it, counting around the last zone to the first. Each value is 8, 16 or 32, one value for each patch of 16 consecutive blocks (patch of block g is g // 16); only the first neighbour_count[b] slots of row b count.
All inputs are finite; a program needn't handle non-finite values.
Results may differ from a plain program's by a relative error of at most 0.007.
The roundings to bfloat16 on the way count: a program that leaves them out, or rounds other values in their place, can miss the bound.
Values may be sent and summed in bfloat16 or wider, within the bound.
No kernel may reach another device: no remote copies, remote signals or barrier semaphores. Data moves between devices by JAX's collectives and lax.ppermute only.
A program may use at most 448 MiB of HBM per device.

v0:
```python
import functools
import math

import jax
import jax.numpy as jnp
from jax import lax
from jax.experimental import pallas as pl
from jax.experimental.pallas import tpu as pltpu
from jax.sharding import PartitionSpec as P


TILE = 128
HEADS = 4
LANES = 128
PAIR = 2 * LANES
AUG = LANES + 16
NEG = -1e30
ATTEND_LIMIT = 20
FINISH_LIMIT = 24
BF = jnp.bfloat16
F32 = jnp.float32


def dot(a, b):
    return jnp.dot(a, b, preferred_element_type=F32)


def dot_t(a, b):
    return lax.dot_general(a, b, (((1,), (1,)), ((), ())), preferred_element_type=F32)


def whole(memory_space=pltpu.VMEM):
    return pl.BlockSpec(memory_space=memory_space)


def query_kernel(own_ref, partner_ref, wq_ref, wv_ref, out_ref, wv_t_ref):
    blocks = own_ref.shape[0] // TILE
    wv_t_ref[...] = wv_ref[...].T
    wq_t = wq_ref[...].T
    for half, ref in enumerate((own_ref, partner_ref)):
        q_t = dot_t(wq_t, ref[...]).astype(BF)
        zero = jnp.zeros((LANES, TILE), BF)
        for b in range(blocks):
            col = slice(b * TILE, (b + 1) * TILE)
            for pair in range(HEADS // 2):
                top = q_t[pair * PAIR : pair * PAIR + LANES, col]
                low = q_t[pair * PAIR + LANES : (pair + 1) * PAIR, col]
                slot = out_ref.at[half * blocks + b, pair]
                slot[:LANES, :LANES] = top
                slot[:LANES, LANES:] = zero
                slot[LANES:, :LANES] = zero
                slot[LANES:, LANES:] = low


def make_queries(own, partner, wq, wv):
    blocks = 2 * own.shape[0] // TILE
    return pl.pallas_call(
        query_kernel,
        out_shape=[
            jax.ShapeDtypeStruct((blocks, HEADS // 2, PAIR, PAIR), BF),
            jax.ShapeDtypeStruct(wv.shape, BF),
        ],
        in_specs=[whole()] * 4,
        out_specs=[whole()] * 2,
        compiler_params=pltpu.CompilerParams(vmem_limit_bytes=16 << 20),
        cost_estimate=pl.CostEstimate(
            flops=2 * 2 * own.shape[0] * own.shape[1] ** 2,
            bytes_accessed=4 << 20,
            transcendentals=0,
        ),
        name="queries",
    )(own, partner, wq, wv)


def table_kernel(plan, blocks, slots, count_ref, valid_ref, own_ref, partner_ref, out_ref, *scratch):
    listed, member, flat, sem = scratch
    groups = plan(lax.axis_index("zone"), lax.axis_index("dev"))
    zone_blocks = blocks * lax.axis_size("dev")
    rows, width = own_ref.shape
    row = lax.broadcasted_iota(jnp.int32, (rows, width), 0)
    lane = lax.broadcasted_iota(jnp.int32, (rows, width), 1)
    count = jnp.zeros((rows, width), jnp.int32)
    for r in range(rows):
        count = jnp.where(row == r, count_ref[r], count)
    listed[:rows, :] = jnp.where(lane < count, own_ref[...], -1)
    listed[rows:, :] = jnp.where(lane < count, partner_ref[...], -1)
    every = listed[...]
    wide = lax.broadcasted_iota(jnp.int32, member.shape, 1)
    found = jnp.zeros(member.shape, jnp.int32)
    k = 0
    ids = []
    for group in groups:
        ids.append([])
        for z, d in group:
            for j in range(blocks):
                block = z * zone_blocks + d * blocks + j
                hit = jnp.max(jnp.where(every == block, 1, 0), axis=1, keepdims=True)
                found = jnp.where(wide == k, hit, found)
                ids[-1].append(block)
                k += 1
    member[...] = found
    copy = pltpu.make_async_copy(member, flat, sem)
    copy.start()
    copy.wait()
    base = 0
    for g, group in enumerate(ids):
        ends = []
        for stream in range(2):
            start = stream * slots
            pos = jnp.int32(start)
            for b in range(blocks):
                for j in range(len(group)):
                    out_ref[g, pos] = j + 256 * b
                    pos = pos + flat[stream * blocks + b, base + j]
                out_ref[g, pos] = out_ref[g, jnp.maximum(pos - 1, start)] + 65536
                pos = pos + pos % 2
            ends.append(pos - start)
        steps = jnp.maximum(ends[0], ends[1]) // 2
        steps = steps + steps % 2
        for stream in range(2):

            def fill(i, carry, g=g, start=stream * slots):
                out_ref[g, start + 2 * i] = 256 * blocks
                out_ref[g, start + 2 * i + 1] = 256 * blocks + 65536
                return carry

            lax.fori_loop(ends[stream] // 2, steps + 1, fill, 0)
        out_ref[g, 2 * slots] = steps
        for j, block in enumerate(group):
            out_ref[g, 2 * slots + 1 + j] = valid_ref[block]
        base += len(group)


def make_tables(plan, sizes, blocks, counts, tile_valid, own, partner):
    slots = blocks * max(sizes) * blocks + 4
    width = 2 * slots + 1 + blocks * max(sizes)
    width += -width % LANES
    keys = sum(sizes) * blocks
    tables = pl.pallas_call(
        functools.partial(table_kernel, plan, blocks, slots),
        out_shape=jax.ShapeDtypeStruct((len(sizes), width), jnp.int32),
        in_specs=[whole(pltpu.SMEM)] * 2 + [whole()] * 2,
        out_specs=whole(pltpu.SMEM),
        scratch_shapes=[
            pltpu.VMEM((2 * blocks, own.shape[1]), jnp.int32),
            pltpu.VMEM((2 * blocks, keys + -keys % LANES), jnp.int32),
            pltpu.SMEM((2 * blocks, keys + -keys % LANES), jnp.int32),
            pltpu.SemaphoreType.DMA,
        ],
        compiler_params=pltpu.CompilerParams(vmem_limit_bytes=8 << 20),
        cost_estimate=pl.CostEstimate(flops=10_000_000, bytes_accessed=1 << 20, transcendentals=0),
        name="tables",
    )(counts, tile_valid, own, partner)
    return tables, slots


def pick_kernel(edge_ref, inner_ref, out_ref):
    chip = lax.axis_index("dev") // 2
    at_edge = (chip == 0) | (chip == lax.axis_size("dev") // 2 - 1)

    @pl.when(at_edge)
    def _():
        out_ref[...] = edge_ref[...]

    @pl.when(jnp.logical_not(at_edge))
    def _():
        out_ref[...] = inner_ref[...]


def pick(at_edge, inner):
    return pl.pallas_call(
        pick_kernel,
        out_shape=jax.ShapeDtypeStruct(inner.shape, inner.dtype),
        in_specs=[whole()] * 2,
        out_specs=whole(),
        compiler_params=pltpu.CompilerParams(vmem_limit_bytes=8 << 20),
        cost_estimate=pl.CostEstimate(flops=0, bytes_accessed=1 << 20, transcendentals=0),
        name="pick",
    )(at_edge, inner)


def attend_kernel(n_slabs, group, slots, blocks, factor, first, *refs):
    table = refs[0]
    slabs = refs[1 : 1 + n_slabs]
    wk_ref, wv_t_ref, q_ref = refs[1 + n_slabs : 4 + n_slabs]
    rest = refs[4 + n_slabs :]
    olds, rest = ([], rest) if first else (rest[:4], rest[4:])
    outs, rest = rest[:4], rest[4:]
    states = ((outs[0], outs[1]), (outs[2], outs[3]))
    k_buf, v_buf, s_even, s_odd, peak_even, peak_odd = rest
    key_blocks = n_slabs * blocks
    if first:
        for acc, top in states:
            acc[...] = jnp.zeros_like(acc)
            top[...] = jnp.full_like(top, NEG)
    for old, out in zip(olds, outs):
        out[...] = old[...]
    v_buf[key_blocks] = jnp.zeros(v_buf.shape[1:], BF)

    def entry(stream, i):
        e0 = table[group, stream * slots + 2 * i]
        e1 = table[group, stream * slots + 2 * i + 1]
        k0, k1 = e0 & 255, e1 & 255
        return (e0 >> 8) & 255, k0, k1, jnp.where(e1 >= 65536, key_blocks, k1)

    for i, x in enumerate(slabs):
        row = lax.broadcasted_iota(jnp.int32, (TILE, x.shape[1]), 0)
        lane = lax.broadcasted_iota(jnp.int32, (AUG - LANES, TILE), 1)
        filled, zeroed = [], []
        for j in range(blocks):
            valid = table[group, 2 * slots + 1 + i * blocks + j]
            keep = jnp.where(row < valid, 1.0, 0.0).astype(BF)
            tile = x[j * TILE : (j + 1) * TILE, :]
            part = tile * keep
            zeroed.append(part)
            filled.append(part + tile[0:1, :] * (1 - keep))
            ones = jnp.where(lane < valid, 1.0, 0.0).astype(BF)
            for h in range(HEADS):
                v_buf[i * blocks + j, h, LANES:, :] = ones
        keys = dot(jnp.concatenate(filled, 0), wk_ref[...]).astype(BF)
        vals = dot_t(wv_t_ref[...], jnp.concatenate(zeroed, 0)).astype(BF)
        for j in range(blocks):
            k_buf[i * blocks + j] = keys[j * TILE : (j + 1) * TILE, :]
            for h in range(HEADS):
                v_buf[i * blocks + j, h, :LANES, :] = vals[
                    h * LANES : (h + 1) * LANES, j * TILE : (j + 1) * TILE
                ]

    def score(i, buf, peaks):
        for stream in range(2):
            b, k0, k1, _ = entry(stream, i)
            qi = jnp.minimum(b, blocks - 1) + stream * blocks
            for pair in range(HEADS // 2):
                cols = slice(pair * PAIR, (pair + 1) * PAIR)
                q = q_ref[qi, pair]
                s0 = dot(k_buf[k0, :, cols], q)
                s1 = dot(k_buf[k1, :, cols], q)
                buf[stream, pair, 0] = s0
                buf[stream, pair, 1] = s1
                peaks[stream, 0:1, cols] = jnp.max(
                    jnp.maximum(s0, s1), axis=0, keepdims=True
                )

    def update(i, buf, peaks):
        for stream, (acc, top) in enumerate(states):
            b, k0, _, v1 = entry(stream, i)
            old = top[b, 0:1, :]
            new = jnp.maximum(old, peaks[stream, 0:1, :])
            scale = jnp.exp2((old - new) * factor)
            top[b, 0:1, :] = new
            for pair in range(HEADS // 2):
                high = new[:, pair * PAIR : (pair + 1) * PAIR]
                p0 = jnp.exp2((buf[stream, pair, 0] - high) * factor).astype(BF)
                p1 = jnp.exp2((buf[stream, pair, 1] - high) * factor).astype(BF)
                for side in range(2):
                    h = pair * 2 + side
                    sub = slice(side * LANES, (side + 1) * LANES)
                    p = jnp.concatenate([p0[:, sub], p1[:, sub]], axis=0)
                    v = jnp.concatenate([v_buf[k0, h], v_buf[v1, h]], axis=1)
                    part = scale[:, h * LANES : (h + 1) * LANES]
                    acc[b, h] = acc[b, h] * part + dot(v, p)

    score(0, s_even, peak_even)

    def two(i, carry):
        score(2 * i + 1, s_odd, peak_odd)
        update(2 * i, s_even, peak_even)
        score(2 * i + 2, s_even, peak_even)
        update(2 * i + 1, s_odd, peak_odd)
        return carry

    lax.fori_loop(0, table[group, 2 * slots] // 2, two, 0)


def attend(slabs, group, tables, wk, wv_t, queries, factor, state):
    table, slots = tables
    rows, width = slabs[0].shape
    blocks = rows // TILE
    n = len(slabs)
    key_blocks = n * blocks
    first = state is None
    state_shapes = [
        jax.ShapeDtypeStruct((blocks + 1, HEADS, AUG, TILE), F32),
        jax.ShapeDtypeStruct((blocks + 1, 8, HEADS * LANES), F32),
    ] * 2
    operands = [table, *slabs, wk, wv_t, queries]
    in_specs = [whole(pltpu.SMEM)] + [whole()] * (n + 3)
    aliases = {}
    if not first:
        aliases = {len(operands) + i: i for i in range(4)}
        operands += list(state)
        in_specs += [whole()] * 4
    return pl.pallas_call(
        functools.partial(attend_kernel, n, group, slots, blocks, factor, first),
        out_shape=state_shapes,
        in_specs=in_specs,
        out_specs=[whole()] * 4,
        input_output_aliases=aliases,
        scratch_shapes=[
            pltpu.VMEM((key_blocks, TILE, width), BF),
            pltpu.VMEM((key_blocks + 1, HEADS, AUG, TILE), BF),
            pltpu.VMEM((2, HEADS // 2, 2, TILE, PAIR), F32),
            pltpu.VMEM((2, HEADS // 2, 2, TILE, PAIR), F32),
            pltpu.VMEM((2, 8, width), F32),
            pltpu.VMEM((2, 8, width), F32),
        ],
        compiler_params=pltpu.CompilerParams(vmem_limit_bytes=ATTEND_LIMIT << 20),
        cost_estimate=pl.CostEstimate(
            flops=n * 2_000_000_000, bytes_accessed=8 << 20, transcendentals=0
        ),
        name="attend",
    )(*operands)


def finish_kernel(
    factor,
    acc_ref,
    top_ref,
    acc2_ref,
    top2_ref,
    x_ref,
    wo_ref,
    wg_ref,
    wu_ref,
    wd_ref,
    out_ref,
    att,
):
    rows, _ = x_ref.shape
    for b in range(rows // TILE):
        for h in range(HEADS):
            cols = slice(h * LANES, (h + 1) * LANES)
            m1 = top_ref[b, 0:1, cols]
            m2 = top2_ref[b, 0:1, cols]
            m = jnp.maximum(m1, m2)
            a1 = jnp.exp2((m1 - m) * factor)
            a2 = jnp.exp2((m2 - m) * factor)
            den = (
                acc_ref[b, h, LANES : LANES + 1, :] * a1
                + acc2_ref[b, h, LANES : LANES + 1, :] * a2
            )
            num = acc_ref[b, h, :LANES, :] * a1 + acc2_ref[b, h, :LANES, :] * a2
            att[b * TILE : (b + 1) * TILE, cols] = (num / den).T.astype(BF)
    residual = x_ref[...].astype(F32) + dot(att[...], wo_ref[...])
    inverse = lax.rsqrt(jnp.mean(residual * residual, axis=-1, keepdims=True) + 1e-06)
    normed = (residual * inverse).astype(BF)
    total = residual
    ff = wg_ref.shape[1]
    for start in range(0, ff, 512):
        cols = slice(start, min(start + 512, ff))
        gate = dot(normed, wg_ref[:, cols])
        up = dot(normed, wu_ref[:, cols])
        hidden = (gate / (1.0 + jnp.exp(-gate)) * up).astype(BF)
        total = total + dot(hidden, wd_ref[cols, :])
    out_ref[...] = total.astype(BF)


def finish(mine, theirs, x, w_out, w_gate, w_up, w_down, factor):
    rows, width = x.shape
    ff = w_gate.shape[1]
    return pl.pallas_call(
        functools.partial(finish_kernel, factor),
        out_shape=jax.ShapeDtypeStruct(x.shape, BF),
        in_specs=[whole()] * 9,
        out_specs=whole(),
        scratch_shapes=[pltpu.VMEM((rows, width), BF)],
        compiler_params=pltpu.CompilerParams(vmem_limit_bytes=FINISH_LIMIT << 20),
        cost_estimate=pl.CostEstimate(
            flops=2 * rows * width * (width + 3 * ff), bytes_accessed=12 << 20, transcendentals=0
        ),
        name="finish",
    )(*mine, *theirs, x, w_out, w_gate, w_up, w_down)


def pairs(zones, devs, move):
    out = []
    for zone in range(zones):
        for dev in range(devs):
            to = move(zone, dev)
            if to is not None:
                out.append((zone * devs + dev, to[0] * devs + to[1]))
    return out


def send(x, zones, devs, move):
    return lax.ppermute(x, ("zone", "dev"), pairs(zones, devs, move))


def walks(zones, devs):
    return zones == 4 and devs == 8


def walk_plan(zone, dev):
    n, f = zone ^ 1, zone ^ 3
    return [
        [(zone, dev)],
        [(zone, dev ^ 2), (n, dev)],
        [(zone, dev ^ 4), (n, dev ^ 2), (f, dev)],
        [(zone, dev ^ 6), (n, dev ^ 4), (f, dev ^ 2)],
        [(n, dev ^ 6), (f, dev ^ 4), (f, dev ^ 6)],
    ]


def walk_links(x, zones, devs, work):
    go = functools.partial(send, zones=zones, devs=devs)
    near = lambda a: go(a, move=lambda z, d: (z ^ 1, d))
    relay = lambda a: go(a, move=lambda z, d: (z ^ 2, d))
    inner = lambda d: d // 2 in (1, 2)
    middle = lambda a: go(a, move=lambda z, d: (z, d ^ 6) if inner(d) else None)
    outer = lambda a: go(a, move=lambda z, d: (z, d ^ 2) if inner(d) else None)
    ends = lambda a: go(a, move=lambda z, d: (z, d ^ 6) if not inner(d) else None)

    a1 = go(x, move=lambda z, d: (z, d ^ 2))
    n0 = near(x)
    p2 = middle(x)
    work([x])
    p4 = outer(p2)
    n1 = near(a1)
    f0 = relay(n0)
    p3 = middle(a1)
    work([a1, n0])
    p5 = outer(p3)
    f1 = relay(n1)
    a2 = pick(p4, p3)
    n2 = near(a2)
    g_inner = middle(f0)
    work([a2, n1, f0])
    a3 = pick(p5, p2)
    n3 = near(a3)
    f2 = relay(n2)
    g_ends = ends(f0)
    work([a3, n2, f1])
    f3 = pick(g_ends, g_inner)
    work([n3, f2, f3])


def gather_plan(zone, dev, zones, devs):
    return [
        [(where, 2 * c + dev % 2) for c in range(start, min(start + 2, devs // 2))]
        for where in (zone, (zone - 1) % zones, (zone + 1) % zones)
        for start in range(0, devs // 2, 2)
    ]


def gather_zones(x, zones, devs, work):
    chips = devs // 2
    ahead = lax.ppermute(x, "zone", [(i, (i + 1) % zones) for i in range(zones)])
    behind = lax.ppermute(x, "zone", [((i + 1) % zones, i) for i in range(zones)])
    same_core = [[d for d in range(devs) if d % 2 == c] for c in range(2)]
    for slab in (x, ahead, behind):
        every = lax.all_gather(slab, "dev", axis=0, axis_index_groups=same_core)
        for start in range(0, chips, 2):
            work([every[c] for c in range(start, min(start + 2, chips))])


def body(
    node_features,
    neighbour_blocks,
    neighbour_count,
    tile_valid,
    w_query,
    w_key,
    w_value,
    w_out,
    w_gate,
    w_up,
    w_down,
):
    rows, width = node_features.shape
    blocks = rows // TILE
    zones, devs = lax.axis_size("zone"), lax.axis_size("dev")
    factor = math.log2(math.e) / math.sqrt(width // HEADS)
    go = functools.partial(send, zones=zones, devs=devs)
    swap = lambda a: go(a, move=lambda z, d: (z, d ^ 1))

    partner = swap(node_features)
    listed = swap(neighbour_blocks)
    if walks(zones, devs):
        plan, run = walk_plan, walk_links
    else:
        plan, run = functools.partial(gather_plan, zones=zones, devs=devs), gather_zones
    sizes = [len(group) for group in plan(0, 0)]
    tables = make_tables(
        plan, sizes, blocks, neighbour_count, tile_valid, neighbour_blocks, listed
    )
    queries, wv_t = make_queries(node_features, partner, w_query, w_value)
    state, turn = None, 0

    def work(slabs):
        nonlocal state, turn
        state = attend(slabs, turn, tables, w_key, wv_t, queries, factor, state)
        turn += 1

    run(node_features, zones, devs, work)
    theirs = [swap(state[2]), swap(state[3])]
    return finish(state[:2], theirs, node_features, w_out, w_gate, w_up, w_down, factor)


def solution(mesh):
    placed = (
        P(("zone", "dev"), None),
        P(("zone", "dev"), None),
        P(("zone", "dev")),
        P(),
        P(),
        P(),
        P(),
        P(),
        P(),
        P(),
        P(),
    )

    return jax.shard_map(
        body, mesh=mesh, in_specs=placed, out_specs=P(("zone", "dev"), None), check_vma=False
    )
```

profile of v0, /device:TPU:0, one launch (start us, length us, event | category | flops | bytes accessed | tf_op | source)
XLA Modules:
  0.0 92.1 jit_solution(7568634251646075524)
XLA Ops:
  0.0 3.1 %collective-permute-start.1 = (bf16[512,512]{1,0:T(8,128)(2,1)}, bf16[512,512]{1,0:T(8,128)(2,1)S(1)}, u32[]{:S(2)}, u32[]{:S(2)}) collective-permute-start(bf16[512,512]{1,0:T(8,128)(2,1)} %x_ref.1), channel_id=1, source_target_pairs={{0,2},{1,3},{2,0},{3,1},{4,6},{5,7},{6,4},{7,5},{8,10},{9,11},{10,... | collective-permute-start | bytes 1572872 | tf_op jit(solution)/shard_map/ppermute | solution.py:386
  3.1 0.7 collective-permute-start.4
  3.7 1.6 %collective-permute-start.9 = (bf16[512,512]{1,0:T(8,128)(2,1)}, bf16[512,512]{1,0:T(8,128)(2,1)S(1)}, u32[]{:S(2)}, u32[]{:S(2)}) collective-permute-start(bf16[512,512]{1,0:T(8,128)(2,1)} %x_ref.1), channel_id=1, source_target_pairs={{0,8},{1,9},{2,10},{3,11},{4,12},{5,13},{6,14},{7,15},{8,0},{9,1},... | collective-permute-start | bytes 1572872 | tf_op jit(solution)/shard_map/ppermute | solution.py:386
  5.3 0.0 collective-permute-start.13
  5.3 0.5 collective-permute-start
  5.8 1.6 %collective-permute-done.partner_ref = s32[4,32]{1,0:T(4,128)S(1)} collective-permute-done((s32[4,32]{1,0:T(4,128)}, s32[4,32]{1,0:T(4,128)S(1)}, u32[]{:S(2)}, u32[]{:S(2)}) %collective-permute-start) | collective-permute-done | bytes 544 | tf_op jit(solution)/shard_map/ppermute | solution.py:386
  7.4 0.0 copy-start.9
  7.4 0.7 copy-done.9
  8.1 0.0 copy-start.10
  8.1 0.7 copy-done.10
  8.8 0.0 copy-start.11
  8.8 0.7 copy-done.11
  9.4 3.7 %tables.1.refs_0_ = s32[5,128]{1,0:T(8,128)S(1)} custom-call(s32[4]{0:T(128)S(1)} %copy-done.10, s32[128]{0:T(128)S(1)} %copy-done.11, s32[4,32]{1,0:T(4,128)S(1)} %copy-done.9, s32[4,32]{1,0:T(4,128)S(1)} %collective-permute-done.partner_ref), custom_call_target="tpu_custom_call" | custom-call | flops 10000000 | bytes 1048576 | tf_op jit(solution)/shard_map/tables/pallas_call | solution.py:139
  13.1 2.1 %collective-permute-done.1.refs_1_ = bf16[512,512]{1,0:T(8,128)(2,1)S(1)} collective-permute-done((bf16[512,512]{1,0:T(8,128)(2,1)}, bf16[512,512]{1,0:T(8,128)(2,1)S(1)}, u32[]{:S(2)}, u32[]{:S(2)}) %collective-permute-start.1) | collective-permute-done | bytes 524320 | tf_op jit(solution)/shard_map/ppermute | solution.py:386
  15.2 0.7 collective-permute-start.2
  15.9 1.7 %collective-permute-start.14 = (bf16[512,512]{1,0:T(8,128)(2,1)S(1)}, bf16[512,512]{1,0:T(8,128)(2,1)S(1)}, u32[]{:S(2)}, u32[]{:S(2)}) collective-permute-start(bf16[512,512]{1,0:T(8,128)(2,1)S(1)} %collective-permute-done.1.refs_1_), channel_id=1, source_target_pairs={{0,8},{1,9},{2,10},{3,11},{4,12},{5,13},{6,14},{7,15},{8,0},{9,1},... | collective-permute-start | bytes 1572872 | tf_op jit(solution)/shard_map/ppermute | solution.py:386
  17.6 0.0 collective-permute-done.4.inner_ref
  17.6 1.3 %collective-permute-start.6 = (bf16[512,512]{1,0:T(8,128)(2,1)S(1)}, bf16[512,512]{1,0:T(8,128)(2,1)S(1)}, u32[]{:S(2)}, u32[]{:S(2)}) collective-permute-start(bf16[512,512]{1,0:T(8,128)(2,1)S(1)} %collective-permute-done.4.inner_ref), channel_id=1, source_target_pairs={{2,0},{3,1},{4,6},{5,7},{10,8},{11,9},{12,14},{13,15},{18,16},{19,... | collective-permute-start | bytes 1572872 | tf_op jit(solution)/shard_map/ppermute | solution.py:386
  18.9 0.0 collective-permute-done.9.refs_2_
  18.9 1.6 %collective-permute-start.10 = (bf16[512,512]{1,0:T(8,128)(2,1)S(1)}, bf16[512,512]{1,0:T(8,128)(2,1)S(1)}, u32[]{:S(2)}, u32[]{:S(2)}) collective-permute-start(bf16[512,512]{1,0:T(8,128)(2,1)S(1)} %collective-permute-done.9.refs_2_), channel_id=1, source_target_pairs={{0,16},{1,17},{2,18},{3,19},{4,20},{5,21},{6,22},{7,23},{8,24},{9,... | collective-permute-start | bytes 1572872 | tf_op jit(solution)/shard_map/ppermute | solution.py:386
  20.5 0.0 collective-permute-done.13.partner_ref
  20.5 0.0 copy-start
  20.5 1.0 %copy-done = bf16[512,512]{1,0:T(8,128)(2,1)S(1)} copy-done((bf16[512,512]{1,0:T(8,128)(2,1)S(1)}, bf16[512,512]{1,0:T(8,128)(2,1)}, u32[]{:S(2)}) %copy-start) | copy-done | bytes 524312
  21.5 0.0 copy-start.1
  21.5 1.0 %copy-done.1 = bf16[512,512]{1,0:T(8,128)(2,1)S(1)} copy-done((bf16[512,512]{1,0:T(8,128)(2,1)S(1)}, bf16[512,512]{1,0:T(8,128)(2,1)}, u32[]{:S(2)}) %copy-start.1) | copy-done | bytes 524312
  22.6 0.0 copy-start.2
  22.6 1.0 %copy-done.2 = bf16[512,512]{1,0:T(8,128)(2,1)S(1)} copy-done((bf16[512,512]{1,0:T(8,128)(2,1)S(1)}, bf16[512,512]{1,0:T(8,128)(2,1)}, u32[]{:S(2)}) %copy-start.2) | copy-done | bytes 524312
  23.6 0.0 copy-start.3
  23.6 0.9 queries.1
  24.5 0.1 copy-done.3
  24.7 0.2 copy-done.7
  24.8 2.7 %attend.5 = (f32[5,4,144,128]{3,2,1,0:T(8,128)S(1)}, f32[5,8,512]{2,1,0:T(8,128)S(1)}, f32[5,4,144,128]{3,2,1,0:T(8,128)S(1)}, f32[5,8,512]{2,1,0:T(8,128)S(1)}) custom-call(s32[5,128]{1,0:T(8,128)S(1)} %tables.1.refs_0_, bf16[512,512]{1,0:T(8,128)(2,1)S(1)} %copy-done.3, bf16[512,512]{1,0:T(8,128)(2,1)S(1)} %copy-done.7, ...), custom_call_target="tpu_custom_call" | custom-call | flops 2000000000 | bytes 8388608 | tf_op jit(solution)/shard_map/attend/pallas_call | solution.py:293
  27.6 4.6 %attend.6 = (f32[5,4,144,128]{3,2,1,0:T(8,128)S(1)}, f32[5,8,512]{2,1,0:T(8,128)S(1)}, f32[5,4,144,128]{3,2,1,0:T(8,128)S(1)}, f32[5,8,512]{2,1,0:T(8,128)S(1)}) custom-call(s32[5,128]{1,0:T(8,128)S(1)} %tables.1.refs_0_, ...), custom_call_target="tpu_custom_call", output_to_operand_aliasing={{0}: (6, {}), {1}: (7, {}), {2}: (8, {}), {3}: (9, {})} | custom-call | flops 4000000000 | bytes 8388608 | tf_op jit(solution)/shard_map/attend/pallas_call | solution.py:293
  32.1 0.0 collective-permute-done.2.inner_ref
  32.1 1.6 %collective-permute-done.6.edge_ref = bf16[512,512]{1,0:T(8,128)(2,1)S(1)} collective-permute-done((bf16[512,512]{1,0:T(8,128)(2,1)S(1)}, bf16[512,512]{1,0:T(8,128)(2,1)S(1)}, u32[]{:S(2)}, u32[]{:S(2)}) %collective-permute-start.6) | collective-permute-done | bytes 524320 | tf_op jit(solution)/shard_map/ppermute | solution.py:386
  33.8 1.0 %collective-permute-start.7 = (bf16[512,512]{1,0:T(8,128)(2,1)S(1)}, bf16[512,512]{1,0:T(8,128)(2,1)S(1)}, u32[]{:S(2)}, u32[]{:S(2)}) collective-permute-start(bf16[512,512]{1,0:T(8,128)(2,1)S(1)} %pick.4.refs_1_), channel_id=1, source_target_pairs={{0,8},{1,9},{2,10},{3,11},{4,12},{5,13},{6,14},{7,15},{8,0},{9,1},... | collective-permute-start | bytes 1572872 | tf_op jit(solution)/shard_map/ppermute | solution.py:386
  34.8 1.3 %collective-permute-start.3 = (bf16[512,512]{1,0:T(8,128)(2,1)S(1)}, bf16[512,512]{1,0:T(8,128)(2,1)S(1)}, u32[]{:S(2)}, u32[]{:S(2)}) collective-permute-start(bf16[512,512]{1,0:T(8,128)(2,1)S(1)} %collective-permute-done.2.inner_ref), channel_id=1, source_target_pairs={{2,0},{3,1},{4,6},{5,7},{10,8},{11,9},{12,14},{13,15},{18,16},{19,... | collective-permute-start | bytes 1572872 | tf_op jit(solution)/shard_map/ppermute | solution.py:386
  36.1 0.0 collective-permute-done.10.refs_3_
  36.1 6.8 %collective-permute-start.11 = (bf16[512,512]{1,0:T(8,128)(2,1)S(1)}, bf16[512,512]{1,0:T(8,128)(2,1)S(1)}, u32[]{:S(2)}, u32[]{:S(2)}) collective-permute-start(bf16[512,512]{1,0:T(8,128)(2,1)S(1)} %collective-permute-done.10.refs_3_), channel_id=1, source_target_pairs={{0,6},{1,7},{6,0},{7,1},{8,14},{9,15},{14,8},{15,9},{16,22},{17,23... | collective-permute-start | bytes 1572872 | tf_op jit(solution)/shard_map/ppermute | solution.py:386
  42.9 0.7 collective-permute-start.12
  43.6 0.0 collective-permute-done.14.refs_2_
  43.6 0.1 collective-permute-start.15
  43.7 5.3 %attend.7 = (f32[5,4,144,128]{3,2,1,0:T(8,128)S(1)}, f32[5,8,512]{2,1,0:T(8,128)S(1)}, f32[5,4,144,128]{3,2,1,0:T(8,128)S(1)}, f32[5,8,512]{2,1,0:T(8,128)S(1)}) custom-call(s32[5,128]{1,0:T(8,128)S(1)} %tables.1.refs_0_, bf16[512,512]{1,0:T(8,128)(2,1)S(1)} %pick.4.refs_1_, ...), custom_call_target="tpu_custom_call", output_to_operand_aliasing={{0}: (7, {}), {1}: (8, {}), {2}: (9, {}), {3}: (10, {})} | custom-call | flops 6000000000 | bytes 8388608 | tf_op jit(solution)/shard_map/attend/pallas_call | solution.py:293
  49.0 12.2 %collective-permute-done.3.edge_ref = bf16[512,512]{1,0:T(8,128)(2,1)S(1)} collective-permute-done((bf16[512,512]{1,0:T(8,128)(2,1)S(1)}, bf16[512,512]{1,0:T(8,128)(2,1)S(1)}, u32[]{:S(2)}, u32[]{:S(2)}) %collective-permute-start.3) | collective-permute-done | bytes 524320 | tf_op jit(solution)/shard_map/ppermute | solution.py:386
  61.2 0.4 collective-permute-start.5
  61.6 0.0 collective-permute-done.7.refs_2_
  61.6 4.8 %collective-permute-start.8 = (bf16[512,512]{1,0:T(8,128)(2,1)S(1)}, bf16[512,512]{1,0:T(8,128)(2,1)S(1)}, u32[]{:S(2)}, u32[]{:S(2)}) collective-permute-start(bf16[512,512]{1,0:T(8,128)(2,1)S(1)} %collective-permute-done.7.refs_2_), channel_id=1, source_target_pairs={{0,16},{1,17},{2,18},{3,19},{4,20},{5,21},{6,22},{7,23},{8,24},{9,... | collective-permute-start | bytes 1572872 | tf_op jit(solution)/shard_map/ppermute | solution.py:386
  66.4 0.0 collective-permute-done.11.edge_ref
  66.4 0.0 collective-permute-done.12.inner_ref
  66.4 0.0 collective-permute-done.15.refs_3_
  66.4 5.1 %attend.8 = (f32[5,4,144,128]{3,2,1,0:T(8,128)S(1)}, f32[5,8,512]{2,1,0:T(8,128)S(1)}, f32[5,4,144,128]{3,2,1,0:T(8,128)S(1)}, f32[5,8,512]{2,1,0:T(8,128)S(1)}) custom-call(s32[5,128]{1,0:T(8,128)S(1)} %tables.1.refs_0_, bf16[512,512]{1,0:T(8,128)(2,1)S(1)} %pick.3.refs_1_, ...), custom_call_target="tpu_custom_call", output_to_operand_aliasing={{0}: (7, {}), {1}: (8, {}), {2}: (9, {}), {3}: (10, {})} | custom-call | flops 6000000000 | bytes 8388608 | tf_op jit(solution)/shard_map/attend/pallas_call | solution.py:293
  71.5 6.8 %collective-permute-done.8.refs_2_ = bf16[512,512]{1,0:T(8,128)(2,1)S(1)} collective-permute-done((bf16[512,512]{1,0:T(8,128)(2,1)S(1)}, bf16[512,512]{1,0:T(8,128)(2,1)S(1)}, u32[]{:S(2)}, u32[]{:S(2)}) %collective-permute-start.8) | collective-permute-done | bytes 524320 | tf_op jit(solution)/shard_map/ppermute | solution.py:386
  78.3 0.0 collective-permute-done.5.refs_1_
  78.3 0.0 copy-start.8
  78.3 4.0 %attend.9 = (f32[5,4,144,128]{3,2,1,0:T(8,128)S(1)}, f32[5,8,512]{2,1,0:T(8,128)S(1)}, f32[5,4,144,128]{3,2,1,0:T(8,128)S(1)}, f32[5,8,512]{2,1,0:T(8,128)S(1)}) custom-call(s32[5,128]{1,0:T(8,128)S(1)} %tables.1.refs_0_, ...), custom_call_target="tpu_custom_call", output_to_operand_aliasing={{0}: (7, {}), {1}: (8, {}), {2}: (9, {}), {3}: (10, {})} | custom-call | flops 6000000000 | bytes 8388608 | tf_op jit(solution)/shard_map/attend/pallas_call | solution.py:293
  82.4 1.5 %collective-permute-start.16 = (f32[5,4,144,128]{3,2,1,0:T(8,128)S(1)}, f32[5,4,144,128]{3,2,1,0:T(8,128)S(1)}, u32[]{:S(2)}, u32[]{:S(2)}) collective-permute-start(f32[5,4,144,128]{3,2,1,0:T(8,128)S(1)} %get-tuple-element.47), channel_id=1, source_target_pairs={{0,1},{1,0},{2,3},{3,2},{4,5},{5,4},{6,7},{7,6},{8,9},{9,8},{10,11... | collective-permute-start | bytes 4423688 | tf_op jit(solution)/shard_map/ppermute | solution.py:386
  83.9 0.1 collective-permute-start.17
  83.9 2.9 %collective-permute-done.17.top2_ref = f32[5,8,512]{2,1,0:T(8,128)S(1)} collective-permute-done((f32[5,8,512]{2,1,0:T(8,128)S(1)}, f32[5,8,512]{2,1,0:T(8,128)S(1)}, u32[]{:S(2)}, u32[]{:S(2)}) %collective-permute-start.17) | collective-permute-done | bytes 81952 | tf_op jit(solution)/shard_map/ppermute | solution.py:386
  86.9 0.0 collective-permute-done.16.acc2_ref
  86.9 0.0 copy-done.4
  86.9 0.0 copy-done.5
  86.9 0.0 copy-done.6
  86.9 0.0 copy-done.8
  86.9 5.2 %finish.1 = bf16[512,512]{1,0:T(8,128)(2,1)} custom-call(f32[5,4,144,128]{3,2,1,0:T(8,128)S(1)} %get-tuple-element.45.acc_ref, f32[5,8,512]{2,1,0:T(8,128)S(1)} %get-tuple-element.46.top_ref, f32[5,4,144,128]{3,2,1,0:T(8,128)S(1)} %collective-permute-done.16.acc2_ref, f32[5,8,512]{2,1,0:T(8,128)S(1)} %collective-permute-done.17.top2_ref, ...), custom_call_target="tpu_custom_call" | custom-call | flops 3489660928 | bytes 12582912 | tf_op jit(solution)/shard_map/finish/pallas_call | solution.py:361
  (7 shorter events, 0.1 us)
Async XLA Ops:
  0.0 15.2 %collective-permute-start.1 = (bf16[512,512]{1,0:T(8,128)(2,1)}, bf16[512,512]{1,0:T(8,128)(2,1)S(1)}, u32[]{:S(2)}, u32[]{:S(2)}) collective-permute-start(bf16[512,512]{1,0:T(8,128)(2,1)} %x_ref.1), channel_id=1, source_target_pairs={{0,2},{1,3},{2,0},{3,1},{4,6},{5,7},{6,4},{7,5},{8,10},{9,11},{10,... | collective-permute-start | bytes 1572872 | tf_op jit(solution)/shard_map/ppermute | solution.py:386
  3.1 14.5 %collective-permute-start.4 = (bf16[512,512]{1,0:T(8,128)(2,1)}, bf16[512,512]{1,0:T(8,128)(2,1)S(1)}, u32[]{:S(2)}, u32[]{:S(2)}) collective-permute-start(bf16[512,512]{1,0:T(8,128)(2,1)} %x_ref.1), channel_id=1, source_target_pairs={{2,4},{3,5},{4,2},{5,3},{10,12},{11,13},{12,10},{13,11},{18,20},{1... | collective-permute-start | bytes 1572872 | tf_op jit(solution)/shard_map/ppermute | solution.py:386
  3.7 15.2 %collective-permute-start.9 = (bf16[512,512]{1,0:T(8,128)(2,1)}, bf16[512,512]{1,0:T(8,128)(2,1)S(1)}, u32[]{:S(2)}, u32[]{:S(2)}) collective-permute-start(bf16[512,512]{1,0:T(8,128)(2,1)} %x_ref.1), channel_id=1, source_target_pairs={{0,8},{1,9},{2,10},{3,11},{4,12},{5,13},{6,14},{7,15},{8,0},{9,1},... | collective-permute-start | bytes 1572872 | tf_op jit(solution)/shard_map/ppermute | solution.py:386
  5.3 15.2 %collective-permute-start.13 = (bf16[512,512]{1,0:T(8,128)(2,1)}, bf16[512,512]{1,0:T(8,128)(2,1)S(1)}, u32[]{:S(2)}, u32[]{:S(2)}) collective-permute-start(bf16[512,512]{1,0:T(8,128)(2,1)} %x_ref.1), channel_id=1, source_target_pairs={{0,1},{1,0},{2,3},{3,2},{4,5},{5,4},{6,7},{7,6},{8,9},{9,8},{10,11... | collective-permute-start | bytes 1572872 | tf_op jit(solution)/shard_map/ppermute | solution.py:386
  5.3 2.1 %collective-permute-start = (s32[4,32]{1,0:T(4,128)}, s32[4,32]{1,0:T(4,128)S(1)}, u32[]{:S(2)}, u32[]{:S(2)}) collective-permute-start(s32[4,32]{1,0:T(4,128)} %own_ref.2), channel_id=1, source_target_pairs={{0,1},{1,0},{2,3},{3,2},{4,5},{5,4},{6,7},{7,6},{8,9},{9,8},{10,11... | collective-permute-start | bytes 1544 | tf_op jit(solution)/shard_map/ppermute | solution.py:386
  7.4 0.7 copy-start.9
  8.1 0.7 copy-start.10
  8.8 0.7 copy-start.11
  15.2 17.0 %collective-permute-start.2 = (bf16[512,512]{1,0:T(8,128)(2,1)S(1)}, bf16[512,512]{1,0:T(8,128)(2,1)S(1)}, u32[]{:S(2)}, u32[]{:S(2)}) collective-permute-start(bf16[512,512]{1,0:T(8,128)(2,1)S(1)} %collective-permute-done.1.refs_1_), channel_id=1, source_target_pairs={{2,4},{3,5},{4,2},{5,3},{10,12},{11,13},{12,10},{13,11},{18,20},{1... | collective-permute-start | bytes 1572872 | tf_op jit(solution)/shard_map/ppermute | solution.py:386
  15.9 27.7 %collective-permute-start.14 = (bf16[512,512]{1,0:T(8,128)(2,1)S(1)}, bf16[512,512]{1,0:T(8,128)(2,1)S(1)}, u32[]{:S(2)}, u32[]{:S(2)}) collective-permute-start(bf16[512,512]{1,0:T(8,128)(2,1)S(1)} %collective-permute-done.1.refs_1_), channel_id=1, source_target_pairs={{0,8},{1,9},{2,10},{3,11},{4,12},{5,13},{6,14},{7,15},{8,0},{9,1},... | collective-permute-start | bytes 1572872 | tf_op jit(solution)/shard_map/ppermute | solution.py:386
  17.6 16.1 %collective-permute-start.6 = (bf16[512,512]{1,0:T(8,128)(2,1)S(1)}, bf16[512,512]{1,0:T(8,128)(2,1)S(1)}, u32[]{:S(2)}, u32[]{:S(2)}) collective-permute-start(bf16[512,512]{1,0:T(8,128)(2,1)S(1)} %collective-permute-done.4.inner_ref), channel_id=1, source_target_pairs={{2,0},{3,1},{4,6},{5,7},{10,8},{11,9},{12,14},{13,15},{18,16},{19,... | collective-permute-start | bytes 1572872 | tf_op jit(solution)/shard_map/ppermute | solution.py:386
  18.9 17.2 %collective-permute-start.10 = (bf16[512,512]{1,0:T(8,128)(2,1)S(1)}, bf16[512,512]{1,0:T(8,128)(2,1)S(1)}, u32[]{:S(2)}, u32[]{:S(2)}) collective-permute-start(bf16[512,512]{1,0:T(8,128)(2,1)S(1)} %collective-permute-done.9.refs_2_), channel_id=1, source_target_pairs={{0,16},{1,17},{2,18},{3,19},{4,20},{5,21},{6,22},{7,23},{8,24},{9,... | collective-permute-start | bytes 1572872 | tf_op jit(solution)/shard_map/ppermute | solution.py:386
  20.5 1.0 %copy-start = (bf16[512,512]{1,0:T(8,128)(2,1)S(1)}, bf16[512,512]{1,0:T(8,128)(2,1)}, u32[]{:S(2)}) copy-start(bf16[512,512]{1,0:T(8,128)(2,1)} %wq_ref.1) | copy-start | bytes 1572868
  21.5 1.0 %copy-start.1 = (bf16[512,512]{1,0:T(8,128)(2,1)S(1)}, bf16[512,512]{1,0:T(8,128)(2,1)}, u32[]{:S(2)}) copy-start(bf16[512,512]{1,0:T(8,128)(2,1)} %wv_ref.1) | copy-start | bytes 1572868
  22.6 1.0 %copy-start.2 = (bf16[512,512]{1,0:T(8,128)(2,1)S(1)}, bf16[512,512]{1,0:T(8,128)(2,1)}, u32[]{:S(2)}) copy-start(bf16[512,512]{1,0:T(8,128)(2,1)} %x_ref.1) | copy-start | bytes 1572868
  23.6 1.0 %copy-start.3 = (bf16[512,512]{1,0:T(8,128)(2,1)S(1)}, bf16[512,512]{1,0:T(8,128)(2,1)}, u32[]{:S(2)}) copy-start(bf16[512,512]{1,0:T(8,128)(2,1)} %x_ref.1) | copy-start | bytes 1572868
  23.6 1.2 %copy-start.7 = (bf16[512,512]{1,0:T(8,128)(2,1)S(1)}, bf16[512,512]{1,0:T(8,128)(2,1)}, u32[]{:S(2)}) copy-start(bf16[512,512]{1,0:T(8,128)(2,1)} %refs_4_.5) | copy-start | bytes 1572868
  33.8 27.8 %collective-permute-start.7 = (bf16[512,512]{1,0:T(8,128)(2,1)S(1)}, bf16[512,512]{1,0:T(8,128)(2,1)S(1)}, u32[]{:S(2)}, u32[]{:S(2)}) collective-permute-start(bf16[512,512]{1,0:T(8,128)(2,1)S(1)} %pick.4.refs_1_), channel_id=1, source_target_pairs={{0,8},{1,9},{2,10},{3,11},{4,12},{5,13},{6,14},{7,15},{8,0},{9,1},... | collective-permute-start | bytes 1572872 | tf_op jit(solution)/shard_map/ppermute | solution.py:386
  34.8 26.4 %collective-permute-start.3 = (bf16[512,512]{1,0:T(8,128)(2,1)S(1)}, bf16[512,512]{1,0:T(8,128)(2,1)S(1)}, u32[]{:S(2)}, u32[]{:S(2)}) collective-permute-start(bf16[512,512]{1,0:T(8,128)(2,1)S(1)} %collective-permute-done.2.inner_ref), channel_id=1, source_target_pairs={{2,0},{3,1},{4,6},{5,7},{10,8},{11,9},{12,14},{13,15},{18,16},{19,... | collective-permute-start | bytes 1572872 | tf_op jit(solution)/shard_map/ppermute | solution.py:386
  36.1 30.3 %collective-permute-start.11 = (bf16[512,512]{1,0:T(8,128)(2,1)S(1)}, bf16[512,512]{1,0:T(8,128)(2,1)S(1)}, u32[]{:S(2)}, u32[]{:S(2)}) collective-permute-start(bf16[512,512]{1,0:T(8,128)(2,1)S(1)} %collective-permute-done.10.refs_3_), channel_id=1, source_target_pairs={{0,6},{1,7},{6,0},{7,1},{8,14},{9,15},{14,8},{15,9},{16,22},{17,23... | collective-permute-start | bytes 1572872 | tf_op jit(solution)/shard_map/ppermute | solution.py:386
  42.9 23.5 %collective-permute-start.12 = (bf16[512,512]{1,0:T(8,128)(2,1)S(1)}, bf16[512,512]{1,0:T(8,128)(2,1)S(1)}, u32[]{:S(2)}, u32[]{:S(2)}) collective-permute-start(bf16[512,512]{1,0:T(8,128)(2,1)S(1)} %collective-permute-done.10.refs_3_), channel_id=1, source_target_pairs={{2,4},{3,5},{4,2},{5,3},{10,12},{11,13},{12,10},{13,11},{18,20},{1... | collective-permute-start | bytes 1572872 | tf_op jit(solution)/shard_map/ppermute | solution.py:386
  43.6 22.8 %collective-permute-start.15 = (bf16[512,512]{1,0:T(8,128)(2,1)S(1)}, bf16[512,512]{1,0:T(8,128)(2,1)S(1)}, u32[]{:S(2)}, u32[]{:S(2)}) collective-permute-start(bf16[512,512]{1,0:T(8,128)(2,1)S(1)} %collective-permute-done.14.refs_2_), channel_id=1, source_target_pairs={{0,16},{1,17},{2,18},{3,19},{4,20},{5,21},{6,22},{7,23},{8,24},{9,... | collective-permute-start | bytes 1572872 | tf_op jit(solution)/shard_map/ppermute | solution.py:386
  61.2 17.1 %collective-permute-start.5 = (bf16[512,512]{1,0:T(8,128)(2,1)S(1)}, bf16[512,512]{1,0:T(8,128)(2,1)S(1)}, u32[]{:S(2)}, u32[]{:S(2)}) collective-permute-start(bf16[512,512]{1,0:T(8,128)(2,1)S(1)} %pick.3.refs_1_), channel_id=1, source_target_pairs={{0,8},{1,9},{2,10},{3,11},{4,12},{5,13},{6,14},{7,15},{8,0},{9,1},... | collective-permute-start | bytes 1572872 | tf_op jit(solution)/shard_map/ppermute | solution.py:386
  61.6 16.7 %collective-permute-start.8 = (bf16[512,512]{1,0:T(8,128)(2,1)S(1)}, bf16[512,512]{1,0:T(8,128)(2,1)S(1)}, u32[]{:S(2)}, u32[]{:S(2)}) collective-permute-start(bf16[512,512]{1,0:T(8,128)(2,1)S(1)} %collective-permute-done.7.refs_2_), channel_id=1, source_target_pairs={{0,16},{1,17},{2,18},{3,19},{4,20},{5,21},{6,22},{7,23},{8,24},{9,... | collective-permute-start | bytes 1572872 | tf_op jit(solution)/shard_map/ppermute | solution.py:386
  78.3 8.6 %copy-start.4 = (bf16[512,2048]{1,0:T(8,128)(2,1)S(1)}, bf16[512,2048]{1,0:T(8,128)(2,1)}, u32[]{:S(2)}) copy-start(bf16[512,2048]{1,0:T(8,128)(2,1)} %wg_ref.1) | copy-start | bytes 6291460
  78.3 8.6 %copy-start.5 = (bf16[512,2048]{1,0:T(8,128)(2,1)S(1)}, bf16[512,2048]{1,0:T(8,128)(2,1)}, u32[]{:S(2)}) copy-start(bf16[512,2048]{1,0:T(8,128)(2,1)} %wu_ref.1) | copy-start | bytes 6291460
  78.3 8.6 %copy-start.6 = (bf16[2048,512]{1,0:T(8,128)(2,1)S(1)}, bf16[2048,512]{1,0:T(8,128)(2,1)}, u32[]{:S(2)}) copy-start(bf16[2048,512]{1,0:T(8,128)(2,1)} %wd_ref.1) | copy-start | bytes 6291460
  78.3 8.6 %copy-start.8 = (bf16[512,512]{1,0:T(8,128)(2,1)S(1)}, bf16[512,512]{1,0:T(8,128)(2,1)}, u32[]{:S(2)}) copy-start(bf16[512,512]{1,0:T(8,128)(2,1)} %wo_ref.1) | copy-start | bytes 1572868
  82.4 4.5 %collective-permute-start.16 = (f32[5,4,144,128]{3,2,1,0:T(8,128)S(1)}, f32[5,4,144,128]{3,2,1,0:T(8,128)S(1)}, u32[]{:S(2)}, u32[]{:S(2)}) collective-permute-start(f32[5,4,144,128]{3,2,1,0:T(8,128)S(1)} %get-tuple-element.47), channel_id=1, source_target_pairs={{0,1},{1,0},{2,3},{3,2},{4,5},{5,4},{6,7},{7,6},{8,9},{9,8},{10,11... | collective-permute-start | bytes 4423688 | tf_op jit(solution)/shard_map/ppermute | solution.py:386
  83.9 3.0 %collective-permute-start.17 = (f32[5,8,512]{2,1,0:T(8,128)S(1)}, f32[5,8,512]{2,1,0:T(8,128)S(1)}, u32[]{:S(2)}, u32[]{:S(2)}) collective-permute-start(f32[5,8,512]{2,1,0:T(8,128)S(1)} %get-tuple-element.48), channel_id=1, source_target_pairs={{0,1},{1,0},{2,3},{3,2},{4,5},{5,4},{6,7},{7,6},{8,9},{9,8},{10,11... | collective-permute-start | bytes 245768 | tf_op jit(solution)/shard_map/ppermute | solution.py:386
where the time goes:
time: 93.8 us; the launch traced here: 92.1 us
  Pallas kernels  31.6 us (34%)
  starting transfers between devices  27.6 us (29%)
  waiting for transfers between devices  27.3 us (29%)
  local copies, waits for them, and re-layouts  5.43 us (6%)
    ppermute x18, starting transfers between devices, send(): return lax.ppermute(x, ('zone', 'dev'), pairs(zones, devs, move))  27.6 us
    ppermute x18, waiting for transfers between devices, send(): return lax.ppermute(x, ('zone', 'dev'), pairs(zones, devs, move))  27.3 us
    pallas_call x5, Pallas kernels, attend(): pl.pallas_call(functools.partial(attend_kernel, n, group, slots, blocks,...  21.7 us
    unnamed x24, local copies, waits for them, and re-layouts  5.43 us
    pallas_call x1, Pallas kernels, finish(): pl.pallas_call(functools.partial(finish_kernel, factor), out_shape=jax.Sh...  5.2 us
    pallas_call x1, Pallas kernels, make_tables(): pl.pallas_call(functools.partial(table_kernel, plan, blocks, slots), out_...  3.65 us
  transfers between devices with their start and end apart: 18, of which 6 were waited for; matrix products, arithmetic and copies ran while one was open for 0% of the time, Pallas kernels for 24%

commit v1 on v0

--- a/solution.py
+++ b/solution.py
@@ -33,53 +33,13 @@
     return pl.BlockSpec(memory_space=memory_space)
 
 
-def query_kernel(own_ref, partner_ref, wq_ref, wv_ref, out_ref, wv_t_ref):
-    blocks = own_ref.shape[0] // TILE
-    wv_t_ref[...] = wv_ref[...].T
-    wq_t = wq_ref[...].T
-    for half, ref in enumerate((own_ref, partner_ref)):
-        q_t = dot_t(wq_t, ref[...]).astype(BF)
-        zero = jnp.zeros((LANES, TILE), BF)
-        for b in range(blocks):
-            col = slice(b * TILE, (b + 1) * TILE)
-            for pair in range(HEADS // 2):
-                top = q_t[pair * PAIR : pair * PAIR + LANES, col]
-                low = q_t[pair * PAIR + LANES : (pair + 1) * PAIR, col]
-                slot = out_ref.at[half * blocks + b, pair]
-                slot[:LANES, :LANES] = top
-                slot[:LANES, LANES:] = zero
-                slot[LANES:, :LANES] = zero
-                slot[LANES:, LANES:] = low
-
-
-def make_queries(own, partner, wq, wv):
-    blocks = 2 * own.shape[0] // TILE
-    return pl.pallas_call(
-        query_kernel,
-        out_shape=[
-            jax.ShapeDtypeStruct((blocks, HEADS // 2, PAIR, PAIR), BF),
-            jax.ShapeDtypeStruct(wv.shape, BF),
-        ],
-        in_specs=[whole()] * 4,
-        out_specs=[whole()] * 2,
-        compiler_params=pltpu.CompilerParams(vmem_limit_bytes=16 << 20),
-        cost_estimate=pl.CostEstimate(
-            flops=2 * 2 * own.shape[0] * own.shape[1] ** 2,
-            bytes_accessed=4 << 20,
-            transcendentals=0,
-        ),
-        name="queries",
-    )(own, partner, wq, wv)
-
-
-def table_kernel(plan, blocks, slots, count_ref, valid_ref, own_ref, partner_ref, out_ref, *scratch):
+def fill_tables(groups, slots, width, blocks, count_ref, valid_ref, own_ref, partner_ref, out_ref, scratch):
     listed, member, flat, sem = scratch
-    groups = plan(lax.axis_index("zone"), lax.axis_index("dev"))
     zone_blocks = blocks * lax.axis_size("dev")
-    rows, width = own_ref.shape
-    row = lax.broadcasted_iota(jnp.int32, (rows, width), 0)
-    lane = lax.broadcasted_iota(jnp.int32, (rows, width), 1)
-    count = jnp.zeros((rows, width), jnp.int32)
+    rows, slots_listed = own_ref.shape
+    row = lax.broadcasted_iota(jnp.int32, (rows, slots_listed), 0)
+    lane = lax.broadcasted_iota(jnp.int32, (rows, slots_listed), 1)
+    count = jnp.zeros((rows, slots_listed), jnp.int32)
     for r in range(rows):
         count = jnp.where(row == r, count_ref[r], count)
     listed[:rows, :] = jnp.where(lane < count, own_ref[...], -1)
@@ -106,52 +66,111 @@
     for g, group in enumerate(ids):
         ends = []
         for stream in range(2):
-            start = stream * slots
+            start = g * width + stream * slots
             pos = jnp.int32(start)
             for b in range(blocks):
                 for j in range(len(group)):
-                    out_ref[g, pos] = j + 256 * b
+                    out_ref[pos] = j + 256 * b
                     pos = pos + flat[stream * blocks + b, base + j]
-                out_ref[g, pos] = out_ref[g, jnp.maximum(pos - 1, start)] + 65536
-                pos = pos + pos % 2
+                out_ref[pos] = out_ref[jnp.maximum(pos - 1, start)] + 65536
+                pos = pos + ((pos - start) & 1)
             ends.append(pos - start)
-        steps = jnp.maximum(ends[0], ends[1]) // 2
-        steps = steps + steps % 2
+        steps = jnp.maximum(ends[0], ends[1]) >> 1
+        steps = steps + (steps & 1)
         for stream in range(2):
 
-            def fill(i, carry, g=g, start=stream * slots):
-                out_ref[g, start + 2 * i] = 256 * blocks
-                out_ref[g, start + 2 * i + 1] = 256 * blocks + 65536
+            def fill(i, carry, start=g * width + stream * slots):
+                out_ref[start + 2 * i] = 256 * blocks
+                out_ref[start + 2 * i + 1] = 256 * blocks + 65536
                 return carry
 
-            lax.fori_loop(ends[stream] // 2, steps + 1, fill, 0)
-        out_ref[g, 2 * slots] = steps
+            lax.fori_loop(ends[stream] >> 1, steps + 1, fill, 0)
+        out_ref[g * width + 2 * slots] = steps
         for j, block in enumerate(group):
-            out_ref[g, 2 * slots + 1 + j] = valid_ref[block]
+            out_ref[g * width + 2 * slots + 1 + j] = valid_ref[block]
         base += len(group)
 
 
-def make_tables(plan, sizes, blocks, counts, tile_valid, own, partner):
+def prepare_kernel(plan, blocks, slots, width, *refs):
+    count_hbm, valid_hbm, own_list_hbm, partner_list_hbm, x_hbm, wq_hbm, wv_hbm, partner_ref = refs[:8]
+    table_ref, out_ref, wv_t_ref = refs[8:11]
+    count, valid, own_list, partner_list, x_ref, wq_ref, wv_ref = refs[11:18]
+    scratch, sems = refs[18:22], refs[22]
+    moves = (
+        (count_hbm, count),
+        (valid_hbm, valid),
+        (own_list_hbm, own_list),
+        (partner_list_hbm, partner_list),
+        (wq_hbm, wq_ref),
+        (x_hbm, x_ref),
+        (wv_hbm, wv_ref),
+    )
+    loads = [pltpu.make_async_copy(a, b, sems.at[i]) for i, (a, b) in enumerate(moves)]
+    for load in loads:
+        load.start()
+    for load in loads[:4]:
+        load.wait()
+    groups = plan(lax.axis_index("zone"), lax.axis_index("dev"))
+    fill_tables(groups, slots, width, blocks, count, valid, own_list, partner_list, table_ref, scratch)
+    for load in loads[4:]:
+        load.wait()
+    wv_t_ref[...] = wv_ref[...].T
+    wq_t = wq_ref[...].T
+    zero = jnp.zeros((LANES, TILE), BF)
+    for half, ref in enumerate((x_ref, partner_ref)):
+        q_t = dot_t(wq_t, ref[...]).astype(BF)
+        for b in range(blocks):
+            col = slice(b * TILE, (b + 1) * TILE)
+            for pair in range(HEADS // 2):
+                slot = out_ref.at[half * blocks + b, pair]
+                slot[:LANES, :LANES] = q_t[pair * PAIR : pair * PAIR + LANES, col]
+                slot[:LANES, LANES:] = zero
+                slot[LANES:, :LANES] = zero
+                slot[LANES:, LANES:] = q_t[pair * PAIR + LANES : (pair + 1) * PAIR, col]
+
+
+def prepare(plan, sizes, counts, tile_valid, listed, partner_listed, x, partner, wq, wv):
+    blocks = x.shape[0] // TILE
     slots = blocks * max(sizes) * blocks + 4
     width = 2 * slots + 1 + blocks * max(sizes)
     width += -width % LANES
     keys = sum(sizes) * blocks
-    tables = pl.pallas_call(
-        functools.partial(table_kernel, plan, blocks, slots),
-        out_shape=jax.ShapeDtypeStruct((len(sizes), width), jnp.int32),
-        in_specs=[whole(pltpu.SMEM)] * 2 + [whole()] * 2,
-        out_specs=whole(pltpu.SMEM),
+    keys += -keys % LANES
+    table, queries, wv_t = pl.pallas_call(
+        functools.partial(prepare_kernel, plan, blocks, slots, width),
+        out_shape=[
+            jax.ShapeDtypeStruct((len(sizes) * width,), jnp.int32),
+            jax.ShapeDtypeStruct((2 * blocks, HEADS // 2, PAIR, PAIR), BF),
+            jax.ShapeDtypeStruct(wv.shape, BF),
+        ],
+        in_specs=[whole(pltpu.HBM)] * 3 + [whole(pl.ANY)] + [whole(pltpu.HBM)] * 3 + [whole()],
+        out_specs=[whole(pltpu.SMEM), whole(), whole()],
         scratch_shapes=[
-            pltpu.VMEM((2 * blocks, own.shape[1]), jnp.int32),
-            pltpu.VMEM((2 * blocks, keys + -keys % LANES), jnp.int32),
-            pltpu.SMEM((2 * blocks, keys + -keys % LANES), jnp.int32),
+            pltpu.SMEM(counts.shape, jnp.int32),
+            pltpu.SMEM(tile_valid.shape, jnp.int32),
+            pltpu.VMEM(listed.shape, jnp.int32),
+            pltpu.VMEM(listed.shape, jnp.int32),
+            pltpu.VMEM(x.shape, BF),
+            pltpu.VMEM(wq.shape, BF),
+            pltpu.VMEM(wv.shape, BF),
+            pltpu.VMEM((2 * blocks, listed.shape[1]), jnp.int32),
+            pltpu.VMEM((2 * blocks, keys), jnp.int32),
+            pltpu.SMEM((2 * blocks, keys), jnp.int32),
             pltpu.SemaphoreType.DMA,
+            pltpu.SemaphoreType.DMA((7,)),
         ],
-        compiler_params=pltpu.CompilerParams(vmem_limit_bytes=8 << 20),
-        cost_estimate=pl.CostEstimate(flops=10_000_000, bytes_accessed=1 << 20, transcendentals=0),
-        name="tables",
-    )(counts, tile_valid, own, partner)
-    return tables, slots
+        compiler_params=pltpu.CompilerParams(vmem_limit_bytes=16 << 20),
+        cost_estimate=pl.CostEstimate(
+            flops=4 * x.shape[0] * x.shape[1] ** 2, bytes_accessed=4 << 20, transcendentals=0
+        ),
+        name="prepare",
+    )(
+        *[pltpu.with_memory_space_constraint(a, pltpu.HBM) for a in (counts, tile_valid, listed)],
+        partner_listed,
+        *[pltpu.with_memory_space_constraint(a, pltpu.HBM) for a in (x, wq, wv)],
+        partner,
+    )
+    return (table, slots, width), queries, wv_t
 
 
 def pick_kernel(edge_ref, inner_ref, out_ref):
@@ -179,13 +198,16 @@
     )(at_edge, inner)
 
 
-def attend_kernel(n_slabs, group, slots, blocks, factor, first, *refs):
+def attend_kernel(n_slabs, base, slots, blocks, factor, first, last, *refs):
     table = refs[0]
     slabs = refs[1 : 1 + n_slabs]
     wk_ref, wv_t_ref, q_ref = refs[1 + n_slabs : 4 + n_slabs]
     rest = refs[4 + n_slabs :]
     olds, rest = ([], rest) if first else (rest[:4], rest[4:])
     outs, rest = rest[:4], rest[4:]
+    if last:
+        half_ref, stat_ref, rest = outs[2], outs[3], rest
+        outs, rest = outs[:2] + rest[:2], rest[2:]
     states = ((outs[0], outs[1]), (outs[2], outs[3]))
     k_buf, v_buf, s_even, s_odd, peak_even, peak_odd = rest
     key_blocks = n_slabs * blocks
@@ -198,8 +220,8 @@
     v_buf[key_blocks] = jnp.zeros(v_buf.shape[1:], BF)
 
     def entry(stream, i):
-        e0 = table[group, stream * slots + 2 * i]
-        e1 = table[group, stream * slots + 2 * i + 1]
+        e0 = table[base + stream * slots + 2 * i]
+        e1 = table[base + stream * slots + 2 * i + 1]
         k0, k1 = e0 & 255, e1 & 255
         return (e0 >> 8) & 255, k0, k1, jnp.where(e1 >= 65536, key_blocks, k1)
 
@@ -208,7 +230,7 @@
         lane = lax.broadcasted_iota(jnp.int32, (AUG - LANES, TILE), 1)
         filled, zeroed = [], []
         for j in range(blocks):
-            valid = table[group, 2 * slots + 1 + i * blocks + j]
+            valid = table[base + 2 * slots + 1 + i * blocks + j]
             keep = jnp.where(row < valid, 1.0, 0.0).astype(BF)
             tile = x[j * TILE : (j + 1) * TILE, :]
             part = tile * keep
@@ -226,54 +248,58 @@
                     h * LANES : (h + 1) * LANES, j * TILE : (j + 1) * TILE
                 ]
 
-    def score(i, buf, peaks):
-        for stream in range(2):
-            b, k0, k1, _ = entry(stream, i)
-            qi = jnp.minimum(b, blocks - 1) + stream * blocks
-            for pair in range(HEADS // 2):
-                cols = slice(pair * PAIR, (pair + 1) * PAIR)
-                q = q_ref[qi, pair]
-                s0 = dot(k_buf[k0, :, cols], q)
-                s1 = dot(k_buf[k1, :, cols], q)
-                buf[stream, pair, 0] = s0
-                buf[stream, pair, 1] = s1
-                peaks[stream, 0:1, cols] = jnp.max(
-                    jnp.maximum(s0, s1), axis=0, keepdims=True
-                )
-
-    def update(i, buf, peaks):
-        for stream, (acc, top) in enumerate(states):
-            b, k0, _, v1 = entry(stream, i)
-            old = top[b, 0:1, :]
-            new = jnp.maximum(old, peaks[stream, 0:1, :])
-            scale = jnp.exp2((old - new) * factor)
-            top[b, 0:1, :] = new
-            for pair in range(HEADS // 2):
-                high = new[:, pair * PAIR : (pair + 1) * PAIR]
-                p0 = jnp.exp2((buf[stream, pair, 0] - high) * factor).astype(BF)
-                p1 = jnp.exp2((buf[stream, pair, 1] - high) * factor).astype(BF)
-                for side in range(2):
-                    h = pair * 2 + side
-                    sub = slice(side * LANES, (side + 1) * LANES)
-                    p = jnp.concatenate([p0[:, sub], p1[:, sub]], axis=0)
-                    v = jnp.concatenate([v_buf[k0, h], v_buf[v1, h]], axis=1)
-                    part = scale[:, h * LANES : (h + 1) * LANES]
-                    acc[b, h] = acc[b, h] * part + dot(v, p)
-
-    score(0, s_even, peak_even)
+    def score(i, buf, peaks, stream, pair):
+        b, k0, k1, _ = entry(stream, i)
+        cols = slice(pair * PAIR, (pair + 1) * PAIR)
+        q = q_ref[jnp.minimum(b, blocks - 1) + stream * blocks, pair]
+        s0 = dot(k_buf[k0, :, cols], q)
+        s1 = dot(k_buf[k1, :, cols], q)
+        buf[stream, pair, 0] = s0
+        buf[stream, pair, 1] = s1
+        peaks[stream, 0:1, cols] = jnp.max(jnp.maximum(s0, s1), axis=0, keepdims=True)
+
+    def update(i, buf, peaks, stream, pair):
+        acc, top = states[stream]
+        b, k0, _, v1 = entry(stream, i)
+        cols = slice(pair * PAIR, (pair + 1) * PAIR)
+        old = top[b, 0:1, cols]
+        new = jnp.maximum(old, peaks[stream, 0:1, cols])
+        scale = jnp.exp2((old - new) * factor)
+        top[b, 0:1, cols] = new
+        p0 = jnp.exp2((buf[stream, pair, 0] - new) * factor).astype(BF)
+        p1 = jnp.exp2((buf[stream, pair, 1] - new) * factor).astype(BF)
+        for side in range(2):
+            h = pair * 2 + side
+            sub = slice(side * LANES, (side + 1) * LANES)
+            p = jnp.concatenate([p0[:, sub], p1[:, sub]], axis=0)
+            v = jnp.concatenate([v_buf[k0, h], v_buf[v1, h]], axis=1)
+            acc[b, h] = acc[b, h] * scale[:, sub] + dot(v, p)
+
+    parts = [(stream, pair) for stream in range(2) for pair in range(HEADS // 2)]
+    for part in parts:
+        score(0, s_even, peak_even, *part)
 
     def two(i, carry):
-        score(2 * i + 1, s_odd, peak_odd)
-        update(2 * i, s_even, peak_even)
-        score(2 * i + 2, s_even, peak_even)
-        update(2 * i + 1, s_odd, peak_odd)
+        for part in parts:
+            score(2 * i + 1, s_odd, peak_odd, *part)
+            update(2 * i, s_even, peak_even, *part)
+        for part in parts:
+            score(2 * i + 2, s_even, peak_even, *part)
+            update(2 * i + 1, s_odd, peak_odd, *part)
         return carry
 
-    lax.fori_loop(0, table[group, 2 * slots] // 2, two, 0)
-
-
-def attend(slabs, group, tables, wk, wv_t, queries, factor, state):
-    table, slots = tables
+    lax.fori_loop(0, table[base + 2 * slots] >> 1, two, 0)
+    if last:
+        acc, top = states[1]
+        for b in range(blocks):
+            stat_ref[b, 0:1, :] = top[b, 0:1, :]
+            for h in range(HEADS):
+                half_ref[b, h] = acc[b, h, :LANES, :].astype(BF)
+                stat_ref[b, 1:2, h * LANES : (h + 1) * LANES] = acc[b, h, LANES : LANES + 1, :]
+
+
+def attend(slabs, group, tables, wk, wv_t, queries, factor, state, last):
+    table, slots, table_width = tables
     rows, width = slabs[0].shape
     blocks = rows // TILE
     n = len(slabs)
@@ -283,20 +309,30 @@
         jax.ShapeDtypeStruct((blocks + 1, HEADS, AUG, TILE), F32),
         jax.ShapeDtypeStruct((blocks + 1, 8, HEADS * LANES), F32),
     ] * 2
+    out_shape, scratch = list(state_shapes), []
+    if last:
+        scratch = [pltpu.VMEM(a.shape, a.dtype) for a in state_shapes[2:]]
+        out_shape[2:] = [
+            jax.ShapeDtypeStruct((blocks, HEADS, LANES, TILE), BF),
+            jax.ShapeDtypeStruct((blocks, 8, HEADS * LANES), F32),
+        ]
     operands = [table, *slabs, wk, wv_t, queries]
     in_specs = [whole(pltpu.SMEM)] + [whole()] * (n + 3)
     aliases = {}
     if not first:
-        aliases = {len(operands) + i: i for i in range(4)}
+        aliases = {len(operands) + i: i for i in range(2 if last else 4)}
         operands += list(state)
         in_specs += [whole()] * 4
     return pl.pallas_call(
-        functools.partial(attend_kernel, n, group, slots, blocks, factor, first),
-        out_shape=state_shapes,
+        functools.partial(
+            attend_kernel, n, group * table_width, slots, blocks, factor, first, last
+        ),
+        out_shape=out_shape,
         in_specs=in_specs,
         out_specs=[whole()] * 4,
         input_output_aliases=aliases,
-        scratch_shapes=[
+        scratch_shapes=scratch
+        + [
             pltpu.VMEM((key_blocks, TILE, width), BF),
             pltpu.VMEM((key_blocks + 1, HEADS, AUG, TILE), BF),
             pltpu.VMEM((2, HEADS // 2, 2, TILE, PAIR), F32),
@@ -316,8 +352,8 @@
     factor,
     acc_ref,
     top_ref,
-    acc2_ref,
-    top2_ref,
+    half_ref,
+    stat_ref,
     x_ref,
     wo_ref,
     wg_ref,
@@ -331,15 +367,12 @@
         for h in range(HEADS):
             cols = slice(h * LANES, (h + 1) * LANES)
             m1 = top_ref[b, 0:1, cols]
-            m2 = top2_ref[b, 0:1, cols]
+            m2 = stat_ref[b, 0:1, cols]
             m = jnp.maximum(m1, m2)
             a1 = jnp.exp2((m1 - m) * factor)
             a2 = jnp.exp2((m2 - m) * factor)
-            den = (
-                acc_ref[b, h, LANES : LANES + 1, :] * a1
-                + acc2_ref[b, h, LANES : LANES + 1, :] * a2
-            )
-            num = acc_ref[b, h, :LANES, :] * a1 + acc2_ref[b, h, :LANES, :] * a2
+            den = acc_ref[b, h, LANES : LANES + 1, :] * a1 + stat_ref[b, 1:2, cols] * a2
+            num = acc_ref[b, h, :LANES, :] * a1 + half_ref[b, h].astype(F32) * a2
             att[b * TILE : (b + 1) * TILE, cols] = (num / den).T.astype(BF)
     residual = x_ref[...].astype(F32) + dot(att[...], wo_ref[...])
     inverse = lax.rsqrt(jnp.mean(residual * residual, axis=-1, keepdims=True) + 1e-06)
@@ -466,8 +499,7 @@
     w_up,
     w_down,
 ):
-    rows, width = node_features.shape
-    blocks = rows // TILE
+    _, width = node_features.shape
     zones, devs = lax.axis_size("zone"), lax.axis_size("dev")
     factor = math.log2(math.e) / math.sqrt(width // HEADS)
     go = functools.partial(send, zones=zones, devs=devs)
@@ -480,15 +512,24 @@
     else:
         plan, run = functools.partial(gather_plan, zones=zones, devs=devs), gather_zones
     sizes = [len(group) for group in plan(0, 0)]
-    tables = make_tables(
-        plan, sizes, blocks, neighbour_count, tile_valid, neighbour_blocks, listed
+    tables, queries, wv_t = prepare(
+        plan,
+        sizes,
+        neighbour_count,
+        tile_valid,
+        neighbour_blocks,
+        listed,
+        node_features,
+        partner,
+        w_query,
+        w_value,
     )
-    queries, wv_t = make_queries(node_features, partner, w_query, w_value)
     state, turn = None, 0
 
     def work(slabs):
         nonlocal state, turn
-        state = attend(slabs, turn, tables, w_key, wv_t, queries, factor, state)
+        last = turn == len(sizes) - 1
+        state = attend(slabs, turn, tables, w_key, wv_t, queries, factor, state, last)
         turn += 1
 
     run(node_features, zones, devs, work)

time: 93.8 us -> 87.7 us (0.935)
  local copies, waits for them, and re-layouts: 5.43 us -> 0.02 us
  waiting for transfers between devices: 27.3 us -> 32.7 us
  starting transfers between devices: 27.6 us -> 24.3 us
  Pallas kernels: 31.6 us -> 29.1 us
    ppermute x18, waiting for transfers between devices: 27.3 us -> 32.7 us  [send(): return lax.ppermute(x, ('zone', 'dev'), pairs(zones, devs, move))]
    unnamed x24 -> x12, local copies, waits for them, and re-layouts: 5.43 us -> 0.02 us
    ppermute x18, starting transfers between devices: 27.6 us -> 24.3 us  [send(): return lax.ppermute(x, ('zone', 'dev'), pairs(zones, devs, move))]
    pallas_call x7 -> x6, Pallas kernels: 26.3 us -> 23.6 us  [the longest x5 20.1 us: attend(): pl.pallas_call(functools.partial(attend_kernel, n, group * table_width, s...]
  transfers between devices with their start and end apart: 18 -> 18, of which waited for: 6 -> 5; matrix products, arithmetic and copies ran while one was open for 0% -> 0% of each run, Pallas kernels for 24% -> 23%
where the time goes in v1:
time: 87.7 us; the launch traced here: 86.4 us
  waiting for transfers between devices  32.7 us (37%)
  Pallas kernels  29.1 us (33%)
  starting transfers between devices  24.3 us (28%)
    ppermute x18, waiting for transfers between devices, send(): return lax.ppermute(x, ('zone', 'dev'), pairs(zones, devs, move))  32.7 us
    ppermute x18, starting transfers between devices, send(): return lax.ppermute(x, ('zone', 'dev'), pairs(zones, devs, move))  24.3 us
    pallas_call x5, Pallas kernels, attend(): pl.pallas_call(functools.partial(attend_kernel, n, group * table_width, s...  20.1 us
    pallas_call x1, Pallas kernels, finish(): pl.pallas_call(functools.partial(finish_kernel, factor), out_shape=jax.Sh...  5.18 us
    pallas_call x1, Pallas kernels, prepare(): pl.pallas_call(functools.partial(prepare_kernel, plan, blocks, slots, wid...  3.52 us
  transfers between devices with their start and end apart: 18, of which 5 were waited for; matrix products, arithmetic and copies ran while one was open for 0% of the time, Pallas kernels for 23%

profile of v1, /device:TPU:0, one launch (start us, length us, event | category | flops | bytes accessed | tf_op | source)
XLA Modules:
  0.0 86.4 jit_solution(12284923951605792659)
XLA Ops:
  0.0 0.0 copy-start
  0.0 0.0 copy-start.4
  0.0 3.1 %collective-permute-start.2 = (bf16[512,512]{1,0:T(8,128)(2,1)}, bf16[512,512]{1,0:T(8,128)(2,1)S(1)}, u32[]{:S(2)}, u32[]{:S(2)}) collective-permute-start(bf16[512,512]{1,0:T(8,128)(2,1)} %x_ref.1), channel_id=1, source_target_pairs={{0,2},{1,3},{2,0},{3,1},{4,6},{5,7},{6,4},{7,5},{8,10},{9,11},{10,... | collective-permute-start | bytes 1572872 | tf_op jit(solution)/shard_map/ppermute | solution.py:419
  3.1 0.7 collective-permute-start.5
  3.7 1.6 %collective-permute-start.10 = (bf16[512,512]{1,0:T(8,128)(2,1)}, bf16[512,512]{1,0:T(8,128)(2,1)S(1)}, u32[]{:S(2)}, u32[]{:S(2)}) collective-permute-start(bf16[512,512]{1,0:T(8,128)(2,1)} %x_ref.1), channel_id=1, source_target_pairs={{0,8},{1,9},{2,10},{3,11},{4,12},{5,13},{6,14},{7,15},{8,0},{9,1},... | collective-permute-start | bytes 1572872 | tf_op jit(solution)/shard_map/ppermute | solution.py:419
  5.3 0.0 collective-permute-start.1
  5.3 0.5 collective-permute-start
  5.8 9.4 %collective-permute-done.2.refs_1_ = bf16[512,512]{1,0:T(8,128)(2,1)S(1)} collective-permute-done((bf16[512,512]{1,0:T(8,128)(2,1)}, bf16[512,512]{1,0:T(8,128)(2,1)S(1)}, u32[]{:S(2)}, u32[]{:S(2)}) %collective-permute-start.2) | collective-permute-done | bytes 524320 | tf_op jit(solution)/shard_map/ppermute | solution.py:419
  15.3 0.7 collective-permute-start.3
  15.9 0.0 collective-permute-done.refs_3_
  16.0 1.7 %collective-permute-start.14 = (bf16[512,512]{1,0:T(8,128)(2,1)S(1)}, bf16[512,512]{1,0:T(8,128)(2,1)S(1)}, u32[]{:S(2)}, u32[]{:S(2)}) collective-permute-start(bf16[512,512]{1,0:T(8,128)(2,1)S(1)} %collective-permute-done.2.refs_1_), channel_id=1, source_target_pairs={{0,8},{1,9},{2,10},{3,11},{4,12},{5,13},{6,14},{7,15},{8,0},{9,1},... | collective-permute-start | bytes 1572872 | tf_op jit(solution)/shard_map/ppermute | solution.py:419
  17.6 0.0 collective-permute-done.5.inner_ref
  17.6 1.3 %collective-permute-start.7 = (bf16[512,512]{1,0:T(8,128)(2,1)S(1)}, bf16[512,512]{1,0:T(8,128)(2,1)S(1)}, u32[]{:S(2)}, u32[]{:S(2)}) collective-permute-start(bf16[512,512]{1,0:T(8,128)(2,1)S(1)} %collective-permute-done.5.inner_ref), channel_id=1, source_target_pairs={{2,0},{3,1},{4,6},{5,7},{10,8},{11,9},{12,14},{13,15},{18,16},{19,... | collective-permute-start | bytes 1572872 | tf_op jit(solution)/shard_map/ppermute | solution.py:419
  18.9 0.0 collective-permute-done.10.refs_2_
  18.9 1.6 %collective-permute-start.11 = (bf16[512,512]{1,0:T(8,128)(2,1)S(1)}, bf16[512,512]{1,0:T(8,128)(2,1)S(1)}, u32[]{:S(2)}, u32[]{:S(2)}) collective-permute-start(bf16[512,512]{1,0:T(8,128)(2,1)S(1)} %collective-permute-done.10.refs_2_), channel_id=1, source_target_pairs={{0,16},{1,17},{2,18},{3,19},{4,20},{5,21},{6,22},{7,23},{8,24},{9,... | collective-permute-start | bytes 1572872 | tf_op jit(solution)/shard_map/ppermute | solution.py:419
  20.5 0.0 collective-permute-done.1.refs_7_
  20.5 3.5 %prepare.1 = (s32[640]{0:T(1024)S(1)}, bf16[8,2,256,256]{3,2,1,0:T(8,128)(2,1)S(1)}, bf16[512,512]{1,0:T(8,128)(2,1)S(1)}) custom-call(s32[4]{0:T(128)} %refs_0_.1, s32[128]{0:T(128)} %refs_1_.2, s32[4,32]{1,0:T(4,128)} %refs_2_.2, s32[4,32]{1,0:T(4,128)S(1)} %collective-permute-done.refs_3_, bf16[512,512]{1,0:T(8,128)(2,1)} %x_ref.1, ...), custom_call_target="tpu_custom_call" | custom-call | flops 536870912 | bytes 4194304 | tf_op jit(solution)/shard_map/prepare/pallas_call | solution.py:139
  24.0 0.0 copy-done
  24.0 0.0 copy-done.4
  24.1 2.6 %attend.5 = (f32[5,4,144,128]{3,2,1,0:T(8,128)S(1)}, f32[5,8,512]{2,1,0:T(8,128)S(1)}, f32[5,4,144,128]{3,2,1,0:T(8,128)S(1)}, f32[5,8,512]{2,1,0:T(8,128)S(1)}) custom-call(s32[640]{0:T(1024)S(1)} %get-tuple-element.28.refs_0_, bf16[512,512]{1,0:T(8,128)(2,1)S(1)} %copy-done, bf16[512,512]{1,0:T(8,128)(2,1)S(1)} %copy-done.4, ...), custom_call_target="tpu_custom_call" | custom-call | flops 2000000000 | bytes 8388608 | tf_op jit(solution)/shard_map/attend/pallas_call | solution.py:326
  26.6 4.2 %attend.6 = (f32[5,4,144,128]{3,2,1,0:T(8,128)S(1)}, f32[5,8,512]{2,1,0:T(8,128)S(1)}, f32[5,4,144,128]{3,2,1,0:T(8,128)S(1)}, f32[5,8,512]{2,1,0:T(8,128)S(1)}) custom-call(s32[640]{0:T(1024)S(1)} %get-tuple-element.28.refs_0_, ...), custom_call_target="tpu_custom_call", output_to_operand_aliasing={{0}: (6, {}), {1}: (7, {}), {2}: (8, {}), {3}: (9, {})} | custom-call | flops 4000000000 | bytes 8388608 | tf_op jit(solution)/shard_map/attend/pallas_call | solution.py:326
  30.9 0.0 collective-permute-done.3.inner_ref
  30.9 2.9 %collective-permute-done.7.edge_ref = bf16[512,512]{1,0:T(8,128)(2,1)S(1)} collective-permute-done((bf16[512,512]{1,0:T(8,128)(2,1)S(1)}, bf16[512,512]{1,0:T(8,128)(2,1)S(1)}, u32[]{:S(2)}, u32[]{:S(2)}) %collective-permute-start.7) | collective-permute-done | bytes 524320 | tf_op jit(solution)/shard_map/ppermute | solution.py:419
  33.8 0.6 collective-permute-start.8
  34.4 1.3 %collective-permute-start.4 = (bf16[512,512]{1,0:T(8,128)(2,1)S(1)}, bf16[512,512]{1,0:T(8,128)(2,1)S(1)}, u32[]{:S(2)}, u32[]{:S(2)}) collective-permute-start(bf16[512,512]{1,0:T(8,128)(2,1)S(1)} %collective-permute-done.3.inner_ref), channel_id=1, source_target_pairs={{2,0},{3,1},{4,6},{5,7},{10,8},{11,9},{12,14},{13,15},{18,16},{19,... | collective-permute-start | bytes 1572872 | tf_op jit(solution)/shard_map/ppermute | solution.py:419
  35.7 0.0 collective-permute-done.11.refs_3_
  35.7 5.4 %collective-permute-start.12 = (bf16[512,512]{1,0:T(8,128)(2,1)S(1)}, bf16[512,512]{1,0:T(8,128)(2,1)S(1)}, u32[]{:S(2)}, u32[]{:S(2)}) collective-permute-start(bf16[512,512]{1,0:T(8,128)(2,1)S(1)} %collective-permute-done.11.refs_3_), channel_id=1, source_target_pairs={{0,6},{1,7},{6,0},{7,1},{8,14},{9,15},{14,8},{15,9},{16,22},{17,23... | collective-permute-start | bytes 1572872 | tf_op jit(solution)/shard_map/ppermute | solution.py:419
  41.1 0.7 collective-permute-start.13
  41.8 0.0 collective-permute-done.14.refs_2_
  41.8 0.1 collective-permute-start.15
  41.9 4.8 %attend.7 = (f32[5,4,144,128]{3,2,1,0:T(8,128)S(1)}, f32[5,8,512]{2,1,0:T(8,128)S(1)}, f32[5,4,144,128]{3,2,1,0:T(8,128)S(1)}, f32[5,8,512]{2,1,0:T(8,128)S(1)}) custom-call(s32[640]{0:T(1024)S(1)} %get-tuple-element.28.refs_0_, bf16[512,512]{1,0:T(8,128)(2,1)S(1)} %pick.4.refs_1_, ...), custom_call_target="tpu_custom_call", output_to_operand_aliasing={{0}: (7, {}), {1}: (8, {}), {2}: (9, {}), {3}: (10, {})} | custom-call | flops 6000000000 | bytes 8388608 | tf_op jit(solution)/shard_map/attend/pallas_call | solution.py:326
  46.7 12.6 %collective-permute-done.4.edge_ref = bf16[512,512]{1,0:T(8,128)(2,1)S(1)} collective-permute-done((bf16[512,512]{1,0:T(8,128)(2,1)S(1)}, bf16[512,512]{1,0:T(8,128)(2,1)S(1)}, u32[]{:S(2)}, u32[]{:S(2)}) %collective-permute-start.4) | collective-permute-done | bytes 524320 | tf_op jit(solution)/shard_map/ppermute | solution.py:419
  59.3 1.2 %collective-permute-start.6 = (bf16[512,512]{1,0:T(8,128)(2,1)S(1)}, bf16[512,512]{1,0:T(8,128)(2,1)S(1)}, u32[]{:S(2)}, u32[]{:S(2)}) collective-permute-start(bf16[512,512]{1,0:T(8,128)(2,1)S(1)} %pick.3.refs_1_), channel_id=1, source_target_pairs={{0,8},{1,9},{2,10},{3,11},{4,12},{5,13},{6,14},{7,15},{8,0},{9,1},... | collective-permute-start | bytes 1572872 | tf_op jit(solution)/shard_map/ppermute | solution.py:419
  60.5 0.0 collective-permute-done.8.refs_2_
  60.5 3.5 %collective-permute-start.9 = (bf16[512,512]{1,0:T(8,128)(2,1)S(1)}, bf16[512,512]{1,0:T(8,128)(2,1)S(1)}, u32[]{:S(2)}, u32[]{:S(2)}) collective-permute-start(bf16[512,512]{1,0:T(8,128)(2,1)S(1)} %collective-permute-done.8.refs_2_), channel_id=1, source_target_pairs={{0,16},{1,17},{2,18},{3,19},{4,20},{5,21},{6,22},{7,23},{8,24},{9,... | collective-permute-start | bytes 1572872 | tf_op jit(solution)/shard_map/ppermute | solution.py:419
  64.0 0.0 collective-permute-done.12.edge_ref
  64.0 0.0 collective-permute-done.13.inner_ref
  64.0 0.2 pick.5.refs_3_
  64.2 0.0 collective-permute-done.15.refs_3_
  64.2 4.8 %attend.8 = (f32[5,4,144,128]{3,2,1,0:T(8,128)S(1)}, f32[5,8,512]{2,1,0:T(8,128)S(1)}, f32[5,4,144,128]{3,2,1,0:T(8,128)S(1)}, f32[5,8,512]{2,1,0:T(8,128)S(1)}) custom-call(s32[640]{0:T(1024)S(1)} %get-tuple-element.28.refs_0_, bf16[512,512]{1,0:T(8,128)(2,1)S(1)} %pick.3.refs_1_, ...), custom_call_target="tpu_custom_call", output_to_operand_aliasing={{0}: (7, {}), {1}: (8, {}), {2}: (9, {}), {3}: (10, {})} | custom-call | flops 6000000000 | bytes 8388608 | tf_op jit(solution)/shard_map/attend/pallas_call | solution.py:326
  69.0 6.3 %collective-permute-done.9.refs_2_ = bf16[512,512]{1,0:T(8,128)(2,1)S(1)} collective-permute-done((bf16[512,512]{1,0:T(8,128)(2,1)S(1)}, bf16[512,512]{1,0:T(8,128)(2,1)S(1)}, u32[]{:S(2)}, u32[]{:S(2)}) %collective-permute-start.9) | collective-permute-done | bytes 524320 | tf_op jit(solution)/shard_map/ppermute | solution.py:419
  75.2 0.0 collective-permute-done.6.refs_1_
  75.2 0.0 copy-start.1
  75.2 0.0 copy-start.2
  75.2 0.0 copy-start.3
  75.2 0.0 copy-start.5
  75.3 3.8 %attend.9 = (f32[5,4,144,128]{3,2,1,0:T(8,128)S(1)}, f32[5,8,512]{2,1,0:T(8,128)S(1)}, bf16[4,4,128,128]{3,2,1,0:T(8,128)(2,1)S(1)}, f32[4,8,512]{2,1,0:T(8,128)S(1)}) custom-call(s32[640]{0:T(1024)S(1)} %get-tuple-element.28.refs_0_, bf16[512,512]{1,0:T(8,128)(2,1)S(1)} %collective-permute-done.6.refs_1_, ...), custom_call_target="tpu_custom_call", output_to_operand_aliasing={{0}: (7, {}), {1}: (8, {})} | custom-call | flops 6000000000 | bytes 8388608 | tf_op jit(solution)/shard_map/attend/pallas_call | solution.py:326
  79.1 0.5 collective-permute-start.16
  79.6 0.1 collective-permute-start.17
  79.7 1.5 %collective-permute-done.17.stat_ref = f32[4,8,512]{2,1,0:T(8,128)S(1)} collective-permute-done((f32[4,8,512]{2,1,0:T(8,128)S(1)}, f32[4,8,512]{2,1,0:T(8,128)S(1)}, u32[]{:S(2)}, u32[]{:S(2)}) %collective-permute-start.17) | collective-permute-done | bytes 65568 | tf_op jit(solution)/shard_map/ppermute | solution.py:419
  81.2 0.0 collective-permute-done.16.half_ref
  81.2 0.0 copy-done.1
  81.2 0.0 copy-done.2
  81.2 0.0 copy-done.3
  81.2 0.0 copy-done.5
  81.2 5.2 %finish.1 = bf16[512,512]{1,0:T(8,128)(2,1)} custom-call(f32[5,4,144,128]{3,2,1,0:T(8,128)S(1)} %get-tuple-element.47.acc_ref, f32[5,8,512]{2,1,0:T(8,128)S(1)} %get-tuple-element.48.top_ref, bf16[4,4,128,128]{3,2,1,0:T(8,128)(2,1)S(1)} %collective-permute-done.16.half_ref, f32[4,8,512]{2,1,0:T(8,128)S(1)} %collective-permute-done.17.stat_ref, ...), custom_call_target="tpu_custom_call" | custom-call | flops 3489660928 | bytes 12582912 | tf_op jit(solution)/shard_map/finish/pallas_call | solution.py:394
  (2 shorter events, 0.1 us)
Async XLA Ops:
  0.0 24.0 %copy-start = (bf16[512,512]{1,0:T(8,128)(2,1)S(1)}, bf16[512,512]{1,0:T(8,128)(2,1)}, u32[]{:S(2)}) copy-start(bf16[512,512]{1,0:T(8,128)(2,1)} %x_ref.1) | copy-start | bytes 1572868
  0.0 24.0 %copy-start.4 = (bf16[512,512]{1,0:T(8,128)(2,1)S(1)}, bf16[512,512]{1,0:T(8,128)(2,1)}, u32[]{:S(2)}) copy-start(bf16[512,512]{1,0:T(8,128)(2,1)} %refs_4_.7) | copy-start | bytes 1572868
  0.0 15.3 %collective-permute-start.2 = (bf16[512,512]{1,0:T(8,128)(2,1)}, bf16[512,512]{1,0:T(8,128)(2,1)S(1)}, u32[]{:S(2)}, u32[]{:S(2)}) collective-permute-start(bf16[512,512]{1,0:T(8,128)(2,1)} %x_ref.1), channel_id=1, source_target_pairs={{0,2},{1,3},{2,0},{3,1},{4,6},{5,7},{6,4},{7,5},{8,10},{9,11},{10,... | collective-permute-start | bytes 1572872 | tf_op jit(solution)/shard_map/ppermute | solution.py:419
  3.1 14.6 %collective-permute-start.5 = (bf16[512,512]{1,0:T(8,128)(2,1)}, bf16[512,512]{1,0:T(8,128)(2,1)S(1)}, u32[]{:S(2)}, u32[]{:S(2)}) collective-permute-start(bf16[512,512]{1,0:T(8,128)(2,1)} %x_ref.1), channel_id=1, source_target_pairs={{2,4},{3,5},{4,2},{5,3},{10,12},{11,13},{12,10},{13,11},{18,20},{1... | collective-permute-start | bytes 1572872 | tf_op jit(solution)/shard_map/ppermute | solution.py:419
  3.7 15.2 %collective-permute-start.10 = (bf16[512,512]{1,0:T(8,128)(2,1)}, bf16[512,512]{1,0:T(8,128)(2,1)S(1)}, u32[]{:S(2)}, u32[]{:S(2)}) collective-permute-start(bf16[512,512]{1,0:T(8,128)(2,1)} %x_ref.1), channel_id=1, source_target_pairs={{0,8},{1,9},{2,10},{3,11},{4,12},{5,13},{6,14},{7,15},{8,0},{9,1},... | collective-permute-start | bytes 1572872 | tf_op jit(solution)/shard_map/ppermute | solution.py:419
  5.3 15.2 %collective-permute-start.1 = (bf16[512,512]{1,0:T(8,128)(2,1)}, bf16[512,512]{1,0:T(8,128)(2,1)S(1)}, u32[]{:S(2)}, u32[]{:S(2)}) collective-permute-start(bf16[512,512]{1,0:T(8,128)(2,1)} %x_ref.1), channel_id=1, source_target_pairs={{0,1},{1,0},{2,3},{3,2},{4,5},{5,4},{6,7},{7,6},{8,9},{9,8},{10,11... | collective-permute-start | bytes 1572872 | tf_op jit(solution)/shard_map/ppermute | solution.py:419
  5.3 10.6 %collective-permute-start = (s32[4,32]{1,0:T(4,128)}, s32[4,32]{1,0:T(4,128)S(1)}, u32[]{:S(2)}, u32[]{:S(2)}) collective-permute-start(s32[4,32]{1,0:T(4,128)} %refs_2_.2), channel_id=1, source_target_pairs={{0,1},{1,0},{2,3},{3,2},{4,5},{5,4},{6,7},{7,6},{8,9},{9,8},{10,11... | collective-permute-start | bytes 1544 | tf_op jit(solution)/shard_map/ppermute | solution.py:419
  15.3 15.6 %collective-permute-start.3 = (bf16[512,512]{1,0:T(8,128)(2,1)S(1)}, bf16[512,512]{1,0:T(8,128)(2,1)S(1)}, u32[]{:S(2)}, u32[]{:S(2)}) collective-permute-start(bf16[512,512]{1,0:T(8,128)(2,1)S(1)} %collective-permute-done.2.refs_1_), channel_id=1, source_target_pairs={{2,4},{3,5},{4,2},{5,3},{10,12},{11,13},{12,10},{13,11},{18,20},{1... | collective-permute-start | bytes 1572872 | tf_op jit(solution)/shard_map/ppermute | solution.py:419
  16.0 25.9 %collective-permute-start.14 = (bf16[512,512]{1,0:T(8,128)(2,1)S(1)}, bf16[512,512]{1,0:T(8,128)(2,1)S(1)}, u32[]{:S(2)}, u32[]{:S(2)}) collective-permute-start(bf16[512,512]{1,0:T(8,128)(2,1)S(1)} %collective-permute-done.2.refs_1_), channel_id=1, source_target_pairs={{0,8},{1,9},{2,10},{3,11},{4,12},{5,13},{6,14},{7,15},{8,0},{9,1},... | collective-permute-start | bytes 1572872 | tf_op jit(solution)/shard_map/ppermute | solution.py:419
  17.6 16.1 %collective-permute-start.7 = (bf16[512,512]{1,0:T(8,128)(2,1)S(1)}, bf16[512,512]{1,0:T(8,128)(2,1)S(1)}, u32[]{:S(2)}, u32[]{:S(2)}) collective-permute-start(bf16[512,512]{1,0:T(8,128)(2,1)S(1)} %collective-permute-done.5.inner_ref), channel_id=1, source_target_pairs={{2,0},{3,1},{4,6},{5,7},{10,8},{11,9},{12,14},{13,15},{18,16},{19,... | collective-permute-start | bytes 1572872 | tf_op jit(solution)/shard_map/ppermute | solution.py:419
  18.9 16.8 %collective-permute-start.11 = (bf16[512,512]{1,0:T(8,128)(2,1)S(1)}, bf16[512,512]{1,0:T(8,128)(2,1)S(1)}, u32[]{:S(2)}, u32[]{:S(2)}) collective-permute-start(bf16[512,512]{1,0:T(8,128)(2,1)S(1)} %collective-permute-done.10.refs_2_), channel_id=1, source_target_pairs={{0,16},{1,17},{2,18},{3,19},{4,20},{5,21},{6,22},{7,23},{8,24},{9,... | collective-permute-start | bytes 1572872 | tf_op jit(solution)/shard_map/ppermute | solution.py:419
  33.8 26.7 %collective-permute-start.8 = (bf16[512,512]{1,0:T(8,128)(2,1)S(1)}, bf16[512,512]{1,0:T(8,128)(2,1)S(1)}, u32[]{:S(2)}, u32[]{:S(2)}) collective-permute-start(bf16[512,512]{1,0:T(8,128)(2,1)S(1)} %pick.4.refs_1_), channel_id=1, source_target_pairs={{0,8},{1,9},{2,10},{3,11},{4,12},{5,13},{6,14},{7,15},{8,0},{9,1},... | collective-permute-start | bytes 1572872 | tf_op jit(solution)/shard_map/ppermute | solution.py:419
  34.4 24.9 %collective-permute-start.4 = (bf16[512,512]{1,0:T(8,128)(2,1)S(1)}, bf16[512,512]{1,0:T(8,128)(2,1)S(1)}, u32[]{:S(2)}, u32[]{:S(2)}) collective-permute-start(bf16[512,512]{1,0:T(8,128)(2,1)S(1)} %collective-permute-done.3.inner_ref), channel_id=1, source_target_pairs={{2,0},{3,1},{4,6},{5,7},{10,8},{11,9},{12,14},{13,15},{18,16},{19,... | collective-permute-start | bytes 1572872 | tf_op jit(solution)/shard_map/ppermute | solution.py:419
  35.7 28.3 %collective-permute-start.12 = (bf16[512,512]{1,0:T(8,128)(2,1)S(1)}, bf16[512,512]{1,0:T(8,128)(2,1)S(1)}, u32[]{:S(2)}, u32[]{:S(2)}) collective-permute-start(bf16[512,512]{1,0:T(8,128)(2,1)S(1)} %collective-permute-done.11.refs_3_), channel_id=1, source_target_pairs={{0,6},{1,7},{6,0},{7,1},{8,14},{9,15},{14,8},{15,9},{16,22},{17,23... | collective-permute-start | bytes 1572872 | tf_op jit(solution)/shard_map/ppermute | solution.py:419
  41.1 22.9 %collective-permute-start.13 = (bf16[512,512]{1,0:T(8,128)(2,1)S(1)}, bf16[512,512]{1,0:T(8,128)(2,1)S(1)}, u32[]{:S(2)}, u32[]{:S(2)}) collective-permute-start(bf16[512,512]{1,0:T(8,128)(2,1)S(1)} %collective-permute-done.11.refs_3_), channel_id=1, source_target_pairs={{2,4},{3,5},{4,2},{5,3},{10,12},{11,13},{12,10},{13,11},{18,20},{1... | collective-permute-start | bytes 1572872 | tf_op jit(solution)/shard_map/ppermute | solution.py:419
  41.8 22.4 %collective-permute-start.15 = (bf16[512,512]{1,0:T(8,128)(2,1)S(1)}, bf16[512,512]{1,0:T(8,128)(2,1)S(1)}, u32[]{:S(2)}, u32[]{:S(2)}) collective-permute-start(bf16[512,512]{1,0:T(8,128)(2,1)S(1)} %collective-permute-done.14.refs_2_), channel_id=1, source_target_pairs={{0,16},{1,17},{2,18},{3,19},{4,20},{5,21},{6,22},{7,23},{8,24},{9,... | collective-permute-start | bytes 1572872 | tf_op jit(solution)/shard_map/ppermute | solution.py:419
  59.3 15.9 %collective-permute-start.6 = (bf16[512,512]{1,0:T(8,128)(2,1)S(1)}, bf16[512,512]{1,0:T(8,128)(2,1)S(1)}, u32[]{:S(2)}, u32[]{:S(2)}) collective-permute-start(bf16[512,512]{1,0:T(8,128)(2,1)S(1)} %pick.3.refs_1_), channel_id=1, source_target_pairs={{0,8},{1,9},{2,10},{3,11},{4,12},{5,13},{6,14},{7,15},{8,0},{9,1},... | collective-permute-start | bytes 1572872 | tf_op jit(solution)/shard_map/ppermute | solution.py:419
  60.5 14.7 %collective-permute-start.9 = (bf16[512,512]{1,0:T(8,128)(2,1)S(1)}, bf16[512,512]{1,0:T(8,128)(2,1)S(1)}, u32[]{:S(2)}, u32[]{:S(2)}) collective-permute-start(bf16[512,512]{1,0:T(8,128)(2,1)S(1)} %collective-permute-done.8.refs_2_), channel_id=1, source_target_pairs={{0,16},{1,17},{2,18},{3,19},{4,20},{5,21},{6,22},{7,23},{8,24},{9,... | collective-permute-start | bytes 1572872 | tf_op jit(solution)/shard_map/ppermute | solution.py:419
  75.2 6.0 %copy-start.1 = (bf16[512,2048]{1,0:T(8,128)(2,1)S(1)}, bf16[512,2048]{1,0:T(8,128)(2,1)}, u32[]{:S(2)}) copy-start(bf16[512,2048]{1,0:T(8,128)(2,1)} %wg_ref.1) | copy-start | bytes 6291460
  75.2 6.0 %copy-start.2 = (bf16[512,2048]{1,0:T(8,128)(2,1)S(1)}, bf16[512,2048]{1,0:T(8,128)(2,1)}, u32[]{:S(2)}) copy-start(bf16[512,2048]{1,0:T(8,128)(2,1)} %wu_ref.1) | copy-start | bytes 6291460
  75.2 6.0 %copy-start.3 = (bf16[2048,512]{1,0:T(8,128)(2,1)S(1)}, bf16[2048,512]{1,0:T(8,128)(2,1)}, u32[]{:S(2)}) copy-start(bf16[2048,512]{1,0:T(8,128)(2,1)} %wd_ref.1) | copy-start | bytes 6291460
  75.2 6.0 %copy-start.5 = (bf16[512,512]{1,0:T(8,128)(2,1)S(1)}, bf16[512,512]{1,0:T(8,128)(2,1)}, u32[]{:S(2)}) copy-start(bf16[512,512]{1,0:T(8,128)(2,1)} %wo_ref.1) | copy-start | bytes 1572868
  79.1 2.1 %collective-permute-start.16 = (bf16[4,4,128,128]{3,2,1,0:T(8,128)(2,1)S(1)}, bf16[4,4,128,128]{3,2,1,0:T(8,128)(2,1)S(1)}, u32[]{:S(2)}, u32[]{:S(2)}) collective-permute-start(bf16[4,4,128,128]{3,2,1,0:T(8,128)(2,1)S(1)} %get-tuple-element.49), channel_id=1, source_target_pairs={{0,1},{1,0},{2,3},{3,2},{4,5},{5,4},{6,7},{7,6},{8,9},{9,8},{10,11... | collective-permute-start | bytes 1572872 | tf_op jit(solution)/shard_map/ppermute | solution.py:419
  79.6 1.6 %collective-permute-start.17 = (f32[4,8,512]{2,1,0:T(8,128)S(1)}, f32[4,8,512]{2,1,0:T(8,128)S(1)}, u32[]{:S(2)}, u32[]{:S(2)}) collective-permute-start(f32[4,8,512]{2,1,0:T(8,128)S(1)} %get-tuple-element.50), channel_id=1, source_target_pairs={{0,1},{1,0},{2,3},{3,2},{4,5},{5,4},{6,7},{7,6},{8,9},{9,8},{10,11... | collective-permute-start | bytes 196616 | tf_op jit(solution)/shard_map/ppermute | solution.py:419

commit v2 on v1

--- a/solution.py
+++ b/solution.py
@@ -430,7 +430,8 @@
         [(zone, dev ^ 2), (n, dev)],
         [(zone, dev ^ 4), (n, dev ^ 2), (f, dev)],
         [(zone, dev ^ 6), (n, dev ^ 4), (f, dev ^ 2)],
-        [(n, dev ^ 6), (f, dev ^ 4), (f, dev ^ 6)],
+        [(n, dev ^ 6), (f, dev ^ 4)],
+        [(f, dev ^ 6)],
     ]
 
 
@@ -463,8 +464,8 @@
     f2 = relay(n2)
     g_ends = ends(f0)
     work([a3, n2, f1])
-    f3 = pick(g_ends, g_inner)
-    work([n3, f2, f3])
+    work([n3, f2])
+    work([pick(g_ends, g_inner)])
 
 
 def gather_plan(zone, dev, zones, devs):

time: 87.7 us -> 90.8 us (1.035)
  the two profiles are of different devices: /device:TPU:0 before, /device:TPU:3 now
where the time goes in v2:
time: 90.8 us; the launch traced here: 90.6 us
  Pallas kernels  35.2 us (39%)
  starting transfers between devices  27.5 us (30%)
  waiting for transfers between devices  27.5 us (30%)
    ppermute x18, starting transfers between devices, send(): return lax.ppermute(x, ('zone', 'dev'), pairs(zones, devs, move))  27.5 us
    ppermute x18, waiting for transfers between devices, send(): return lax.ppermute(x, ('zone', 'dev'), pairs(zones, devs, move))  27.5 us
    pallas_call x6, Pallas kernels, attend(): pl.pallas_call(functools.partial(attend_kernel, n, group * table_width, s...  26.2 us
    pallas_call x1, Pallas kernels, finish(): pl.pallas_call(functools.partial(finish_kernel, factor), out_shape=jax.Sh...  5.2 us
    pallas_call x1, Pallas kernels, prepare(): pl.pallas_call(functools.partial(prepare_kernel, plan, blocks, slots, wid...  3.57 us
  transfers between devices with their start and end apart: 18, of which 5 were waited for; matrix products, arithmetic and copies ran while one was open for 0% of the time, Pallas kernels for 24%

profile of v2, /device:TPU:3, one launch (start us, length us, event | category | flops | bytes accessed | tf_op | source)
XLA Modules:
  0.0 90.6 jit_solution(4703109032017006795)
XLA Ops:
  0.0 0.0 copy-start
  0.0 0.0 copy-start.4
  0.0 1.3 %collective-permute-start.6 = (bf16[512,512]{1,0:T(8,128)(2,1)}, bf16[512,512]{1,0:T(8,128)(2,1)S(1)}, u32[]{:S(2)}, u32[]{:S(2)}) collective-permute-start(bf16[512,512]{1,0:T(8,128)(2,1)} %x_ref.1), channel_id=1, source_target_pairs={{0,2},{1,3},{2,0},{3,1},{4,6},{5,7},{6,4},{7,5},{8,10},{9,11},{10,... | collective-permute-start | bytes 1572872 | tf_op jit(solution)/shard_map/ppermute | solution.py:419
  1.3 0.7 collective-permute-start.9
  2.0 0.3 collective-permute-start.2
  2.3 1.2 %collective-permute-start.1 = (bf16[512,512]{1,0:T(8,128)(2,1)}, bf16[512,512]{1,0:T(8,128)(2,1)S(1)}, u32[]{:S(2)}, u32[]{:S(2)}) collective-permute-start(bf16[512,512]{1,0:T(8,128)(2,1)} %x_ref.1), channel_id=1, source_target_pairs={{0,1},{1,0},{2,3},{3,2},{4,5},{5,4},{6,7},{7,6},{8,9},{9,8},{10,11... | collective-permute-start | bytes 1572872 | tf_op jit(solution)/shard_map/ppermute | solution.py:419
  3.5 0.0 collective-permute-start
  3.6 9.5 %collective-permute-done.6.refs_1_ = bf16[512,512]{1,0:T(8,128)(2,1)S(1)} collective-permute-done((bf16[512,512]{1,0:T(8,128)(2,1)}, bf16[512,512]{1,0:T(8,128)(2,1)S(1)}, u32[]{:S(2)}, u32[]{:S(2)}) %collective-permute-start.6) | collective-permute-done | bytes 524320 | tf_op jit(solution)/shard_map/ppermute | solution.py:419
  13.0 0.7 collective-permute-start.7
  13.7 0.0 collective-permute-done.refs_3_
  13.7 0.5 collective-permute-start.14
  14.2 0.0 collective-permute-done.9.inner_ref
  14.2 1.3 %collective-permute-start.11 = (bf16[512,512]{1,0:T(8,128)(2,1)S(1)}, bf16[512,512]{1,0:T(8,128)(2,1)S(1)}, u32[]{:S(2)}, u32[]{:S(2)}) collective-permute-start(bf16[512,512]{1,0:T(8,128)(2,1)S(1)} %collective-permute-done.9.inner_ref), channel_id=1, source_target_pairs={{2,0},{3,1},{4,6},{5,7},{10,8},{11,9},{12,14},{13,15},{18,16},{19,... | collective-permute-start | bytes 1572872 | tf_op jit(solution)/shard_map/ppermute | solution.py:419
  15.5 0.0 collective-permute-done.2.refs_2_
  15.5 1.1 %collective-permute-start.3 = (bf16[512,512]{1,0:T(8,128)(2,1)S(1)}, bf16[512,512]{1,0:T(8,128)(2,1)S(1)}, u32[]{:S(2)}, u32[]{:S(2)}) collective-permute-start(bf16[512,512]{1,0:T(8,128)(2,1)S(1)} %collective-permute-done.2.refs_2_), channel_id=1, source_target_pairs={{0,16},{1,17},{2,18},{3,19},{4,20},{5,21},{6,22},{7,23},{8,24},{9,... | collective-permute-start | bytes 1572872 | tf_op jit(solution)/shard_map/ppermute | solution.py:419
  16.7 0.0 collective-permute-done.1.refs_7_
  16.7 3.6 %prepare.1 = (s32[768]{0:T(1024)S(1)}, bf16[8,2,256,256]{3,2,1,0:T(8,128)(2,1)S(1)}, bf16[512,512]{1,0:T(8,128)(2,1)S(1)}) custom-call(s32[4]{0:T(128)} %refs_0_.1, s32[128]{0:T(128)} %refs_1_.2, s32[4,32]{1,0:T(4,128)} %refs_2_.3, s32[4,32]{1,0:T(4,128)S(1)} %collective-permute-done.refs_3_, bf16[512,512]{1,0:T(8,128)(2,1)} %x_ref.1, ...), custom_call_target="tpu_custom_call" | custom-call | flops 536870912 | bytes 4194304 | tf_op jit(solution)/shard_map/prepare/pallas_call | solution.py:139
  20.2 0.0 copy-done
  20.2 0.0 copy-done.4
  20.3 2.6 %attend.6 = (f32[5,4,144,128]{3,2,1,0:T(8,128)S(1)}, f32[5,8,512]{2,1,0:T(8,128)S(1)}, f32[5,4,144,128]{3,2,1,0:T(8,128)S(1)}, f32[5,8,512]{2,1,0:T(8,128)S(1)}) custom-call(s32[768]{0:T(1024)S(1)} %get-tuple-element.32.refs_0_, bf16[512,512]{1,0:T(8,128)(2,1)S(1)} %copy-done, bf16[512,512]{1,0:T(8,128)(2,1)S(1)} %copy-done.4, ...), custom_call_target="tpu_custom_call" | custom-call | flops 2000000000 | bytes 8388608 | tf_op jit(solution)/shard_map/attend/pallas_call | solution.py:326
  22.8 5.2 %attend.7 = (f32[5,4,144,128]{3,2,1,0:T(8,128)S(1)}, f32[5,8,512]{2,1,0:T(8,128)S(1)}, f32[5,4,144,128]{3,2,1,0:T(8,128)S(1)}, f32[5,8,512]{2,1,0:T(8,128)S(1)}) custom-call(s32[768]{0:T(1024)S(1)} %get-tuple-element.32.refs_0_, ...), custom_call_target="tpu_custom_call", output_to_operand_aliasing={{0}: (6, {}), {1}: (7, {}), {2}: (8, {}), {3}: (9, {})} | custom-call | flops 4000000000 | bytes 8388608 | tf_op jit(solution)/shard_map/attend/pallas_call | solution.py:326
  28.0 0.0 collective-permute-done.7.inner_ref
  28.0 1.3 %collective-permute-done.11.edge_ref = bf16[512,512]{1,0:T(8,128)(2,1)S(1)} collective-permute-done((bf16[512,512]{1,0:T(8,128)(2,1)S(1)}, bf16[512,512]{1,0:T(8,128)(2,1)S(1)}, u32[]{:S(2)}, u32[]{:S(2)}) %collective-permute-start.11) | collective-permute-done | bytes 524320 | tf_op jit(solution)/shard_map/ppermute | solution.py:419
  29.4 1.3 %collective-permute-start.12 = (bf16[512,512]{1,0:T(8,128)(2,1)S(1)}, bf16[512,512]{1,0:T(8,128)(2,1)S(1)}, u32[]{:S(2)}, u32[]{:S(2)}) collective-permute-start(bf16[512,512]{1,0:T(8,128)(2,1)S(1)} %pick.5.refs_1_), channel_id=1, source_target_pairs={{0,8},{1,9},{2,10},{3,11},{4,12},{5,13},{6,14},{7,15},{8,0},{9,1},... | collective-permute-start | bytes 1572872 | tf_op jit(solution)/shard_map/ppermute | solution.py:419
  30.7 1.3 %collective-permute-start.8 = (bf16[512,512]{1,0:T(8,128)(2,1)S(1)}, bf16[512,512]{1,0:T(8,128)(2,1)S(1)}, u32[]{:S(2)}, u32[]{:S(2)}) collective-permute-start(bf16[512,512]{1,0:T(8,128)(2,1)S(1)} %collective-permute-done.7.inner_ref), channel_id=1, source_target_pairs={{2,0},{3,1},{4,6},{5,7},{10,8},{11,9},{12,14},{13,15},{18,16},{19,... | collective-permute-start | bytes 1572872 | tf_op jit(solution)/shard_map/ppermute | solution.py:419
  31.9 0.0 collective-permute-done.3.refs_3_
  31.9 6.5 %collective-permute-start.4 = (bf16[512,512]{1,0:T(8,128)(2,1)S(1)}, bf16[512,512]{1,0:T(8,128)(2,1)S(1)}, u32[]{:S(2)}, u32[]{:S(2)}) collective-permute-start(bf16[512,512]{1,0:T(8,128)(2,1)S(1)} %collective-permute-done.3.refs_3_), channel_id=1, source_target_pairs={{0,6},{1,7},{6,0},{7,1},{8,14},{9,15},{14,8},{15,9},{16,22},{17,23... | collective-permute-start | bytes 1572872 | tf_op jit(solution)/shard_map/ppermute | solution.py:419
  38.5 0.7 collective-permute-start.5
  39.2 0.0 collective-permute-done.14.refs_2_
  39.2 0.1 collective-permute-start.15
  39.3 5.7 %attend.8 = (f32[5,4,144,128]{3,2,1,0:T(8,128)S(1)}, f32[5,8,512]{2,1,0:T(8,128)S(1)}, f32[5,4,144,128]{3,2,1,0:T(8,128)S(1)}, f32[5,8,512]{2,1,0:T(8,128)S(1)}) custom-call(s32[768]{0:T(1024)S(1)} %get-tuple-element.32.refs_0_, bf16[512,512]{1,0:T(8,128)(2,1)S(1)} %pick.5.refs_1_, ...), custom_call_target="tpu_custom_call", output_to_operand_aliasing={{0}: (7, {}), {1}: (8, {}), {2}: (9, {}), {3}: (10, {})} | custom-call | flops 6000000000 | bytes 8388608 | tf_op jit(solution)/shard_map/attend/pallas_call | solution.py:326
  45.0 9.3 %collective-permute-done.8.edge_ref = bf16[512,512]{1,0:T(8,128)(2,1)S(1)} collective-permute-done((bf16[512,512]{1,0:T(8,128)(2,1)S(1)}, bf16[512,512]{1,0:T(8,128)(2,1)S(1)}, u32[]{:S(2)}, u32[]{:S(2)}) %collective-permute-start.8) | collective-permute-done | bytes 524320 | tf_op jit(solution)/shard_map/ppermute | solution.py:419
  54.3 1.3 %collective-permute-start.10 = (bf16[512,512]{1,0:T(8,128)(2,1)S(1)}, bf16[512,512]{1,0:T(8,128)(2,1)S(1)}, u32[]{:S(2)}, u32[]{:S(2)}) collective-permute-start(bf16[512,512]{1,0:T(8,128)(2,1)S(1)} %pick.4.refs_1_), channel_id=1, source_target_pairs={{0,8},{1,9},{2,10},{3,11},{4,12},{5,13},{6,14},{7,15},{8,0},{9,1},... | collective-permute-start | bytes 1572872 | tf_op jit(solution)/shard_map/ppermute | solution.py:419
  55.6 0.0 collective-permute-done.12.refs_2_
  55.6 6.2 %collective-permute-start.13 = (bf16[512,512]{1,0:T(8,128)(2,1)S(1)}, bf16[512,512]{1,0:T(8,128)(2,1)S(1)}, u32[]{:S(2)}, u32[]{:S(2)}) collective-permute-start(bf16[512,512]{1,0:T(8,128)(2,1)S(1)} %collective-permute-done.12.refs_2_), channel_id=1, source_target_pairs={{0,16},{1,17},{2,18},{3,19},{4,20},{5,21},{6,22},{7,23},{8,24},{9,... | collective-permute-start | bytes 1572872 | tf_op jit(solution)/shard_map/ppermute | solution.py:419
  61.8 0.0 collective-permute-done.4.edge_ref
  61.8 0.0 collective-permute-done.5.inner_ref
  61.8 0.2 pick.3.refs_1_
  62.1 0.0 collective-permute-done.15.refs_3_
  62.1 4.8 %attend.9 = (f32[5,4,144,128]{3,2,1,0:T(8,128)S(1)}, f32[5,8,512]{2,1,0:T(8,128)S(1)}, f32[5,4,144,128]{3,2,1,0:T(8,128)S(1)}, f32[5,8,512]{2,1,0:T(8,128)S(1)}) custom-call(s32[768]{0:T(1024)S(1)} %get-tuple-element.32.refs_0_, bf16[512,512]{1,0:T(8,128)(2,1)S(1)} %pick.4.refs_1_, ...), custom_call_target="tpu_custom_call", output_to_operand_aliasing={{0}: (7, {}), {1}: (8, {}), {2}: (9, {}), {3}: (10, {})} | custom-call | flops 6000000000 | bytes 8388608 | tf_op jit(solution)/shard_map/attend/pallas_call | solution.py:326
  66.9 5.9 %collective-permute-done.13.refs_2_ = bf16[512,512]{1,0:T(8,128)(2,1)S(1)} collective-permute-done((bf16[512,512]{1,0:T(8,128)(2,1)S(1)}, bf16[512,512]{1,0:T(8,128)(2,1)S(1)}, u32[]{:S(2)}, u32[]{:S(2)}) %collective-permute-start.13) | collective-permute-done | bytes 524320 | tf_op jit(solution)/shard_map/ppermute | solution.py:419
  72.7 0.0 collective-permute-done.10.refs_1_
  72.7 4.3 %attend.10 = (f32[5,4,144,128]{3,2,1,0:T(8,128)S(1)}, f32[5,8,512]{2,1,0:T(8,128)S(1)}, f32[5,4,144,128]{3,2,1,0:T(8,128)S(1)}, f32[5,8,512]{2,1,0:T(8,128)S(1)}) custom-call(s32[768]{0:T(1024)S(1)} %get-tuple-element.32.refs_0_, ...), custom_call_target="tpu_custom_call", output_to_operand_aliasing={{0}: (6, {}), {1}: (7, {}), {2}: (8, {}), {3}: (9, {})} | custom-call | flops 4000000000 | bytes 8388608 | tf_op jit(solution)/shard_map/attend/pallas_call | solution.py:326
  77.0 0.0 copy-start.1
  77.0 0.0 copy-start.2
  77.1 0.0 copy-start.3
  77.1 0.0 copy-start.5
  77.1 3.6 %attend.11 = (f32[5,4,144,128]{3,2,1,0:T(8,128)S(1)}, f32[5,8,512]{2,1,0:T(8,128)S(1)}, bf16[4,4,128,128]{3,2,1,0:T(8,128)(2,1)S(1)}, f32[4,8,512]{2,1,0:T(8,128)S(1)}) custom-call(s32[768]{0:T(1024)S(1)} %get-tuple-element.32.refs_0_, bf16[512,512]{1,0:T(8,128)(2,1)S(1)} %pick.3.refs_1_, ...), custom_call_target="tpu_custom_call", output_to_operand_aliasing={{0}: (5, {}), {1}: (6, {})} | custom-call | flops 2000000000 | bytes 8388608 | tf_op jit(solution)/shard_map/attend/pallas_call | solution.py:326
  80.7 3.0 %collective-permute-start.16 = (bf16[4,4,128,128]{3,2,1,0:T(8,128)(2,1)S(1)}, bf16[4,4,128,128]{3,2,1,0:T(8,128)(2,1)S(1)}, u32[]{:S(2)}, u32[]{:S(2)}) collective-permute-start(bf16[4,4,128,128]{3,2,1,0:T(8,128)(2,1)S(1)} %get-tuple-element.57), channel_id=1, source_target_pairs={{0,1},{1,0},{2,3},{3,2},{4,5},{5,4},{6,7},{7,6},{8,9},{9,8},{10,11... | collective-permute-start | bytes 1572872 | tf_op jit(solution)/shard_map/ppermute | solution.py:419
  83.7 0.1 collective-permute-start.17
  83.8 1.6 %collective-permute-done.17.stat_ref = f32[4,8,512]{2,1,0:T(8,128)S(1)} collective-permute-done((f32[4,8,512]{2,1,0:T(8,128)S(1)}, f32[4,8,512]{2,1,0:T(8,128)S(1)}, u32[]{:S(2)}, u32[]{:S(2)}) %collective-permute-start.17) | collective-permute-done | bytes 65568 | tf_op jit(solution)/shard_map/ppermute | solution.py:419
  85.3 0.0 collective-permute-done.16.half_ref
  85.3 0.0 copy-done.1
  85.3 0.0 copy-done.2
  85.3 0.0 copy-done.3
  85.3 0.0 copy-done.5
  85.4 5.2 %finish.1 = bf16[512,512]{1,0:T(8,128)(2,1)} custom-call(f32[5,4,144,128]{3,2,1,0:T(8,128)S(1)} %get-tuple-element.55.acc_ref, f32[5,8,512]{2,1,0:T(8,128)S(1)} %get-tuple-element.56.top_ref, bf16[4,4,128,128]{3,2,1,0:T(8,128)(2,1)S(1)} %collective-permute-done.16.half_ref, f32[4,8,512]{2,1,0:T(8,128)S(1)} %collective-permute-done.17.stat_ref, ...), custom_call_target="tpu_custom_call" | custom-call | flops 3489660928 | bytes 12582912 | tf_op jit(solution)/shard_map/finish/pallas_call | solution.py:394
  (2 shorter events, 0.1 us)
Async XLA Ops:
  0.0 20.2 %copy-start = (bf16[512,512]{1,0:T(8,128)(2,1)S(1)}, bf16[512,512]{1,0:T(8,128)(2,1)}, u32[]{:S(2)}) copy-start(bf16[512,512]{1,0:T(8,128)(2,1)} %x_ref.1) | copy-start | bytes 1572868
  0.0 20.2 %copy-start.4 = (bf16[512,512]{1,0:T(8,128)(2,1)S(1)}, bf16[512,512]{1,0:T(8,128)(2,1)}, u32[]{:S(2)}) copy-start(bf16[512,512]{1,0:T(8,128)(2,1)} %refs_2_.5) | copy-start | bytes 1572868
  0.0 13.0 %collective-permute-start.6 = (bf16[512,512]{1,0:T(8,128)(2,1)}, bf16[512,512]{1,0:T(8,128)(2,1)S(1)}, u32[]{:S(2)}, u32[]{:S(2)}) collective-permute-start(bf16[512,512]{1,0:T(8,128)(2,1)} %x_ref.1), channel_id=1, source_target_pairs={{0,2},{1,3},{2,0},{3,1},{4,6},{5,7},{6,4},{7,5},{8,10},{9,11},{10,... | collective-permute-start | bytes 1572872 | tf_op jit(solution)/shard_map/ppermute | solution.py:419
  1.3 12.9 %collective-permute-start.9 = (bf16[512,512]{1,0:T(8,128)(2,1)}, bf16[512,512]{1,0:T(8,128)(2,1)S(1)}, u32[]{:S(2)}, u32[]{:S(2)}) collective-permute-start(bf16[512,512]{1,0:T(8,128)(2,1)} %x_ref.1), channel_id=1, source_target_pairs={{2,4},{3,5},{4,2},{5,3},{10,12},{11,13},{12,10},{13,11},{18,20},{1... | collective-permute-start | bytes 1572872 | tf_op jit(solution)/shard_map/ppermute | solution.py:419
  2.0 13.5 %collective-permute-start.2 = (bf16[512,512]{1,0:T(8,128)(2,1)}, bf16[512,512]{1,0:T(8,128)(2,1)S(1)}, u32[]{:S(2)}, u32[]{:S(2)}) collective-permute-start(bf16[512,512]{1,0:T(8,128)(2,1)} %x_ref.1), channel_id=1, source_target_pairs={{0,8},{1,9},{2,10},{3,11},{4,12},{5,13},{6,14},{7,15},{8,0},{9,1},... | collective-permute-start | bytes 1572872 | tf_op jit(solution)/shard_map/ppermute | solution.py:419
  2.3 14.3 %collective-permute-start.1 = (bf16[512,512]{1,0:T(8,128)(2,1)}, bf16[512,512]{1,0:T(8,128)(2,1)S(1)}, u32[]{:S(2)}, u32[]{:S(2)}) collective-permute-start(bf16[512,512]{1,0:T(8,128)(2,1)} %x_ref.1), channel_id=1, source_target_pairs={{0,1},{1,0},{2,3},{3,2},{4,5},{5,4},{6,7},{7,6},{8,9},{9,8},{10,11... | collective-permute-start | bytes 1572872 | tf_op jit(solution)/shard_map/ppermute | solution.py:419
  3.5 10.2 %collective-permute-start = (s32[4,32]{1,0:T(4,128)}, s32[4,32]{1,0:T(4,128)S(1)}, u32[]{:S(2)}, u32[]{:S(2)}) collective-permute-start(s32[4,32]{1,0:T(4,128)} %refs_2_.3), channel_id=1, source_target_pairs={{0,1},{1,0},{2,3},{3,2},{4,5},{5,4},{6,7},{7,6},{8,9},{9,8},{10,11... | collective-permute-start | bytes 1544 | tf_op jit(solution)/shard_map/ppermute | solution.py:419
  13.0 15.0 %collective-permute-start.7 = (bf16[512,512]{1,0:T(8,128)(2,1)S(1)}, bf16[512,512]{1,0:T(8,128)(2,1)S(1)}, u32[]{:S(2)}, u32[]{:S(2)}) collective-permute-start(bf16[512,512]{1,0:T(8,128)(2,1)S(1)} %collective-permute-done.6.refs_1_), channel_id=1, source_target_pairs={{2,4},{3,5},{4,2},{5,3},{10,12},{11,13},{12,10},{13,11},{18,20},{1... | collective-permute-start | bytes 1572872 | tf_op jit(solution)/shard_map/ppermute | solution.py:419
  13.7 25.5 %collective-permute-start.14 = (bf16[512,512]{1,0:T(8,128)(2,1)S(1)}, bf16[512,512]{1,0:T(8,128)(2,1)S(1)}, u32[]{:S(2)}, u32[]{:S(2)}) collective-permute-start(bf16[512,512]{1,0:T(8,128)(2,1)S(1)} %collective-permute-done.6.refs_1_), channel_id=1, source_target_pairs={{0,8},{1,9},{2,10},{3,11},{4,12},{5,13},{6,14},{7,15},{8,0},{9,1},... | collective-permute-start | bytes 1572872 | tf_op jit(solution)/shard_map/ppermute | solution.py:419
  14.2 15.1 %collective-permute-start.11 = (bf16[512,512]{1,0:T(8,128)(2,1)S(1)}, bf16[512,512]{1,0:T(8,128)(2,1)S(1)}, u32[]{:S(2)}, u32[]{:S(2)}) collective-permute-start(bf16[512,512]{1,0:T(8,128)(2,1)S(1)} %collective-permute-done.9.inner_ref), channel_id=1, source_target_pairs={{2,0},{3,1},{4,6},{5,7},{10,8},{11,9},{12,14},{13,15},{18,16},{19,... | collective-permute-start | bytes 1572872 | tf_op jit(solution)/shard_map/ppermute | solution.py:419
  15.5 16.4 %collective-permute-start.3 = (bf16[512,512]{1,0:T(8,128)(2,1)S(1)}, bf16[512,512]{1,0:T(8,128)(2,1)S(1)}, u32[]{:S(2)}, u32[]{:S(2)}) collective-permute-start(bf16[512,512]{1,0:T(8,128)(2,1)S(1)} %collective-permute-done.2.refs_2_), channel_id=1, source_target_pairs={{0,16},{1,17},{2,18},{3,19},{4,20},{5,21},{6,22},{7,23},{8,24},{9,... | collective-permute-start | bytes 1572872 | tf_op jit(solution)/shard_map/ppermute | solution.py:419
  29.4 26.2 %collective-permute-start.12 = (bf16[512,512]{1,0:T(8,128)(2,1)S(1)}, bf16[512,512]{1,0:T(8,128)(2,1)S(1)}, u32[]{:S(2)}, u32[]{:S(2)}) collective-permute-start(bf16[512,512]{1,0:T(8,128)(2,1)S(1)} %pick.5.refs_1_), channel_id=1, source_target_pairs={{0,8},{1,9},{2,10},{3,11},{4,12},{5,13},{6,14},{7,15},{8,0},{9,1},... | collective-permute-start | bytes 1572872 | tf_op jit(solution)/shard_map/ppermute | solution.py:419
  30.7 23.7 %collective-permute-start.8 = (bf16[512,512]{1,0:T(8,128)(2,1)S(1)}, bf16[512,512]{1,0:T(8,128)(2,1)S(1)}, u32[]{:S(2)}, u32[]{:S(2)}) collective-permute-start(bf16[512,512]{1,0:T(8,128)(2,1)S(1)} %collective-permute-done.7.inner_ref), channel_id=1, source_target_pairs={{2,0},{3,1},{4,6},{5,7},{10,8},{11,9},{12,14},{13,15},{18,16},{19,... | collective-permute-start | bytes 1572872 | tf_op jit(solution)/shard_map/ppermute | solution.py:419
  31.9 29.9 %collective-permute-start.4 = (bf16[512,512]{1,0:T(8,128)(2,1)S(1)}, bf16[512,512]{1,0:T(8,128)(2,1)S(1)}, u32[]{:S(2)}, u32[]{:S(2)}) collective-permute-start(bf16[512,512]{1,0:T(8,128)(2,1)S(1)} %collective-permute-done.3.refs_3_), channel_id=1, source_target_pairs={{0,6},{1,7},{6,0},{7,1},{8,14},{9,15},{14,8},{15,9},{16,22},{17,23... | collective-permute-start | bytes 1572872 | tf_op jit(solution)/shard_map/ppermute | solution.py:419
  38.5 23.3 %collective-permute-start.5 = (bf16[512,512]{1,0:T(8,128)(2,1)S(1)}, bf16[512,512]{1,0:T(8,128)(2,1)S(1)}, u32[]{:S(2)}, u32[]{:S(2)}) collective-permute-start(bf16[512,512]{1,0:T(8,128)(2,1)S(1)} %collective-permute-done.3.refs_3_), channel_id=1, source_target_pairs={{2,4},{3,5},{4,2},{5,3},{10,12},{11,13},{12,10},{13,11},{18,20},{1... | collective-permute-start | bytes 1572872 | tf_op jit(solution)/shard_map/ppermute | solution.py:419
  39.2 22.9 %collective-permute-start.15 = (bf16[512,512]{1,0:T(8,128)(2,1)S(1)}, bf16[512,512]{1,0:T(8,128)(2,1)S(1)}, u32[]{:S(2)}, u32[]{:S(2)}) collective-permute-start(bf16[512,512]{1,0:T(8,128)(2,1)S(1)} %collective-permute-done.14.refs_2_), channel_id=1, source_target_pairs={{0,16},{1,17},{2,18},{3,19},{4,20},{5,21},{6,22},{7,23},{8,24},{9,... | collective-permute-start | bytes 1572872 | tf_op jit(solution)/shard_map/ppermute | solution.py:419
  54.3 18.4 %collective-permute-start.10 = (bf16[512,512]{1,0:T(8,128)(2,1)S(1)}, bf16[512,512]{1,0:T(8,128)(2,1)S(1)}, u32[]{:S(2)}, u32[]{:S(2)}) collective-permute-start(bf16[512,512]{1,0:T(8,128)(2,1)S(1)} %pick.4.refs_1_), channel_id=1, source_target_pairs={{0,8},{1,9},{2,10},{3,11},{4,12},{5,13},{6,14},{7,15},{8,0},{9,1},... | collective-permute-start | bytes 1572872 | tf_op jit(solution)/shard_map/ppermute | solution.py:419
  55.6 17.1 %collective-permute-start.13 = (bf16[512,512]{1,0:T(8,128)(2,1)S(1)}, bf16[512,512]{1,0:T(8,128)(2,1)S(1)}, u32[]{:S(2)}, u32[]{:S(2)}) collective-permute-start(bf16[512,512]{1,0:T(8,128)(2,1)S(1)} %collective-permute-done.12.refs_2_), channel_id=1, source_target_pairs={{0,16},{1,17},{2,18},{3,19},{4,20},{5,21},{6,22},{7,23},{8,24},{9,... | collective-permute-start | bytes 1572872 | tf_op jit(solution)/shard_map/ppermute | solution.py:419
  77.0 8.3 %copy-start.1 = (bf16[512,2048]{1,0:T(8,128)(2,1)S(1)}, bf16[512,2048]{1,0:T(8,128)(2,1)}, u32[]{:S(2)}) copy-start(bf16[512,2048]{1,0:T(8,128)(2,1)} %wg_ref.1) | copy-start | bytes 6291460
  77.0 8.3 %copy-start.2 = (bf16[512,2048]{1,0:T(8,128)(2,1)S(1)}, bf16[512,2048]{1,0:T(8,128)(2,1)}, u32[]{:S(2)}) copy-start(bf16[512,2048]{1,0:T(8,128)(2,1)} %wu_ref.1) | copy-start | bytes 6291460
  77.1 8.3 %copy-start.3 = (bf16[2048,512]{1,0:T(8,128)(2,1)S(1)}, bf16[2048,512]{1,0:T(8,128)(2,1)}, u32[]{:S(2)}) copy-start(bf16[2048,512]{1,0:T(8,128)(2,1)} %wd_ref.1) | copy-start | bytes 6291460
  77.1 8.3 %copy-start.5 = (bf16[512,512]{1,0:T(8,128)(2,1)S(1)}, bf16[512,512]{1,0:T(8,128)(2,1)}, u32[]{:S(2)}) copy-start(bf16[512,512]{1,0:T(8,128)(2,1)} %wo_ref.1) | copy-start | bytes 1572868
  80.7 4.6 %collective-permute-start.16 = (bf16[4,4,128,128]{3,2,1,0:T(8,128)(2,1)S(1)}, bf16[4,4,128,128]{3,2,1,0:T(8,128)(2,1)S(1)}, u32[]{:S(2)}, u32[]{:S(2)}) collective-permute-start(bf16[4,4,128,128]{3,2,1,0:T(8,128)(2,1)S(1)} %get-tuple-element.57), channel_id=1, source_target_pairs={{0,1},{1,0},{2,3},{3,2},{4,5},{5,4},{6,7},{7,6},{8,9},{9,8},{10,11... | collective-permute-start | bytes 1572872 | tf_op jit(solution)/shard_map/ppermute | solution.py:419
  83.7 1.6 %collective-permute-start.17 = (f32[4,8,512]{2,1,0:T(8,128)S(1)}, f32[4,8,512]{2,1,0:T(8,128)S(1)}, u32[]{:S(2)}, u32[]{:S(2)}) collective-permute-start(f32[4,8,512]{2,1,0:T(8,128)S(1)} %get-tuple-element.58), channel_id=1, source_target_pairs={{0,1},{1,0},{2,3},{3,2},{4,5},{5,4},{6,7},{7,6},{8,9},{9,8},{10,11... | collective-permute-start | bytes 196616 | tf_op jit(solution)/shard_map/ppermute | solution.py:419

commit v3 on v2

--- a/solution.py
+++ b/solution.py
@@ -76,7 +76,6 @@
                 pos = pos + ((pos - start) & 1)
             ends.append(pos - start)
         steps = jnp.maximum(ends[0], ends[1]) >> 1
-        steps = steps + (steps & 1)
         for stream in range(2):
 
             def fill(i, carry, start=g * width + stream * slots):
@@ -215,8 +214,14 @@
         for acc, top in states:
             acc[...] = jnp.zeros_like(acc)
             top[...] = jnp.full_like(top, NEG)
-    for old, out in zip(olds, outs):
-        out[...] = old[...]
+    chunks = [
+        (old, out, j) for old, out in zip(olds, outs) for j in range(old.shape[0])
+    ]
+
+    def carry_over(i):
+        for old, out, j in chunks[i :: 2 * n_slabs]:
+            out[j] = old[j]
+
     v_buf[key_blocks] = jnp.zeros(v_buf.shape[1:], BF)
 
     def entry(stream, i):
@@ -240,7 +245,9 @@
             for h in range(HEADS):
                 v_buf[i * blocks + j, h, LANES:, :] = ones
         keys = dot(jnp.concatenate(filled, 0), wk_ref[...]).astype(BF)
+        carry_over(2 * i)
         vals = dot_t(wv_t_ref[...], jnp.concatenate(zeroed, 0)).astype(BF)
+        carry_over(2 * i + 1)
         for j in range(blocks):
             k_buf[i * blocks + j] = keys[j * TILE : (j + 1) * TILE, :]
             for h in range(HEADS):
@@ -280,15 +287,22 @@
         score(0, s_even, peak_even, *part)
 
     def two(i, carry):
-        for part in parts:
-            score(2 * i + 1, s_odd, peak_odd, *part)
+        for before, part in zip(parts[-1:] + parts[:-1], parts):
+            score(2 * i + 1, s_odd, peak_odd, *before)
             update(2 * i, s_even, peak_even, *part)
-        for part in parts:
-            score(2 * i + 2, s_even, peak_even, *part)
+        for before, part in zip(parts[-1:] + parts[:-1], parts):
+            score(2 * i + 2, s_even, peak_even, *before)
             update(2 * i + 1, s_odd, peak_odd, *part)
         return carry
 
-    lax.fori_loop(0, table[base + 2 * slots] >> 1, two, 0)
+    steps = table[base + 2 * slots]
+    lax.fori_loop(0, steps >> 1, two, 0)
+
+    @pl.when((steps & 1) == 1)
+    def _():
+        for part in parts:
+            update(steps - 1, s_even, peak_even, *part)
+
     if last:
         acc, top = states[1]
         for b in range(blocks):
@@ -426,8 +440,7 @@
 def walk_plan(zone, dev):
     n, f = zone ^ 1, zone ^ 3
     return [
-        [(zone, dev)],
-        [(zone, dev ^ 2), (n, dev)],
+        [(zone, dev), (zone, dev ^ 2), (n, dev)],
         [(zone, dev ^ 4), (n, dev ^ 2), (f, dev)],
         [(zone, dev ^ 6), (n, dev ^ 4), (f, dev ^ 2)],
         [(n, dev ^ 6), (f, dev ^ 4)],
@@ -447,12 +460,11 @@
     a1 = go(x, move=lambda z, d: (z, d ^ 2))
     n0 = near(x)
     p2 = middle(x)
-    work([x])
     p4 = outer(p2)
     n1 = near(a1)
     f0 = relay(n0)
     p3 = middle(a1)
-    work([a1, n0])
+    work([x, a1, n0])
     p5 = outer(p3)
     f1 = relay(n1)
     a2 = pick(p4, p3)

time: 90.8 us -> 84.4 us (0.930)
  the two profiles are of different devices: /device:TPU:3 before, /device:TPU:0 now
where the time goes in v3:
time: 84.4 us; the launch traced here: 83.9 us
  waiting for transfers between devices  32.8 us (39%)
  Pallas kernels  28.2 us (33%)
  starting transfers between devices  22.6 us (27%)
    ppermute x18, waiting for transfers between devices, send(): return lax.ppermute(x, ('zone', 'dev'), pairs(zones, devs, move))  32.8 us
    ppermute x18, starting transfers between devices, send(): return lax.ppermute(x, ('zone', 'dev'), pairs(zones, devs, move))  22.6 us
    pallas_call x5, Pallas kernels, attend(): pl.pallas_call(functools.partial(attend_kernel, n, group * table_width, s...  19.3 us
    pallas_call x1, Pallas kernels, finish(): pl.pallas_call(functools.partial(finish_kernel, factor), out_shape=jax.Sh...  5.2 us
    pallas_call x1, Pallas kernels, prepare(): pl.pallas_call(functools.partial(prepare_kernel, plan, blocks, slots, wid...  3.46 us
  transfers between devices with their start and end apart: 18, of which 5 were waited for; matrix products, arithmetic and copies ran while one was open for 0% of the time, Pallas kernels for 21%

profile of v3, /device:TPU:0, one launch (start us, length us, event | category | flops | bytes accessed | tf_op | source)
XLA Modules:
  0.0 83.9 jit_solution(601699186722513024)
XLA Ops:
  0.0 0.0 copy-start
  0.0 0.0 copy-start.4
  0.0 3.1 %collective-permute-start.6 = (bf16[512,512]{1,0:T(8,128)(2,1)}, bf16[512,512]{1,0:T(8,128)(2,1)S(1)}, u32[]{:S(2)}, u32[]{:S(2)}) collective-permute-start(bf16[512,512]{1,0:T(8,128)(2,1)} %x_ref.1), channel_id=1, source_target_pairs={{0,2},{1,3},{2,0},{3,1},{4,6},{5,7},{6,4},{7,5},{8,10},{9,11},{10,... | collective-permute-start | bytes 1572872 | tf_op jit(solution)/shard_map/ppermute | solution.py:433
  3.1 0.7 collective-permute-start.9
  3.7 1.6 %collective-permute-start.2 = (bf16[512,512]{1,0:T(8,128)(2,1)}, bf16[512,512]{1,0:T(8,128)(2,1)S(1)}, u32[]{:S(2)}, u32[]{:S(2)}) collective-permute-start(bf16[512,512]{1,0:T(8,128)(2,1)} %x_ref.1), channel_id=1, source_target_pairs={{0,8},{1,9},{2,10},{3,11},{4,12},{5,13},{6,14},{7,15},{8,0},{9,1},... | collective-permute-start | bytes 1572872 | tf_op jit(solution)/shard_map/ppermute | solution.py:433
  5.3 0.0 collective-permute-start.1
  5.3 0.5 collective-permute-start
  5.8 9.4 %collective-permute-done.6.refs_2_ = bf16[512,512]{1,0:T(8,128)(2,1)S(1)} collective-permute-done((bf16[512,512]{1,0:T(8,128)(2,1)}, bf16[512,512]{1,0:T(8,128)(2,1)S(1)}, u32[]{:S(2)}, u32[]{:S(2)}) %collective-permute-start.6) | collective-permute-done | bytes 524320 | tf_op jit(solution)/shard_map/ppermute | solution.py:433
  15.3 0.7 collective-permute-start.7
  15.9 0.0 collective-permute-done.refs_3_
  16.0 1.7 %collective-permute-start.14 = (bf16[512,512]{1,0:T(8,128)(2,1)S(1)}, bf16[512,512]{1,0:T(8,128)(2,1)S(1)}, u32[]{:S(2)}, u32[]{:S(2)}) collective-permute-start(bf16[512,512]{1,0:T(8,128)(2,1)S(1)} %collective-permute-done.6.refs_2_), channel_id=1, source_target_pairs={{0,8},{1,9},{2,10},{3,11},{4,12},{5,13},{6,14},{7,15},{8,0},{9,1},... | collective-permute-start | bytes 1572872 | tf_op jit(solution)/shard_map/ppermute | solution.py:433
  17.6 0.0 collective-permute-done.9.inner_ref
  17.6 1.3 %collective-permute-start.11 = (bf16[512,512]{1,0:T(8,128)(2,1)S(1)}, bf16[512,512]{1,0:T(8,128)(2,1)S(1)}, u32[]{:S(2)}, u32[]{:S(2)}) collective-permute-start(bf16[512,512]{1,0:T(8,128)(2,1)S(1)} %collective-permute-done.9.inner_ref), channel_id=1, source_target_pairs={{2,0},{3,1},{4,6},{5,7},{10,8},{11,9},{12,14},{13,15},{18,16},{19,... | collective-permute-start | bytes 1572872 | tf_op jit(solution)/shard_map/ppermute | solution.py:433
  18.9 0.0 collective-permute-done.2.refs_3_
  18.9 1.6 %collective-permute-start.3 = (bf16[512,512]{1,0:T(8,128)(2,1)S(1)}, bf16[512,512]{1,0:T(8,128)(2,1)S(1)}, u32[]{:S(2)}, u32[]{:S(2)}) collective-permute-start(bf16[512,512]{1,0:T(8,128)(2,1)S(1)} %collective-permute-done.2.refs_3_), channel_id=1, source_target_pairs={{0,16},{1,17},{2,18},{3,19},{4,20},{5,21},{6,22},{7,23},{8,24},{9,... | collective-permute-start | bytes 1572872 | tf_op jit(solution)/shard_map/ppermute | solution.py:433
  20.5 0.0 collective-permute-done.1.refs_7_
  20.5 3.5 %prepare.1 = (s32[640]{0:T(1024)S(1)}, bf16[8,2,256,256]{3,2,1,0:T(8,128)(2,1)S(1)}, bf16[512,512]{1,0:T(8,128)(2,1)S(1)}) custom-call(s32[4]{0:T(128)} %refs_0_.1, s32[128]{0:T(128)} %refs_1_.2, s32[4,32]{1,0:T(4,128)} %refs_2_.2, s32[4,32]{1,0:T(4,128)S(1)} %collective-permute-done.refs_3_, bf16[512,512]{1,0:T(8,128)(2,1)} %x_ref.1, ...), custom_call_target="tpu_custom_call" | custom-call | flops 536870912 | bytes 4194304 | tf_op jit(solution)/shard_map/prepare/pallas_call | solution.py:138
  24.0 0.0 copy-done
  24.0 0.0 copy-done.4
  24.0 4.6 %attend.5 = (f32[5,4,144,128]{3,2,1,0:T(8,128)S(1)}, f32[5,8,512]{2,1,0:T(8,128)S(1)}, f32[5,4,144,128]{3,2,1,0:T(8,128)S(1)}, f32[5,8,512]{2,1,0:T(8,128)S(1)}) custom-call(s32[640]{0:T(1024)S(1)} %get-tuple-element.28.refs_0_, bf16[512,512]{1,0:T(8,128)(2,1)S(1)} %copy-done, bf16[512,512]{1,0:T(8,128)(2,1)S(1)} %collective-permute-done.6.refs_2_, ...), custom_call_target="tpu_custom_call" | custom-call | flops 6000000000 | bytes 8388608 | tf_op jit(solution)/shard_map/attend/pallas_call | solution.py:340
  28.6 0.0 collective-permute-done.7.inner_ref
  28.6 5.2 %collective-permute-done.11.edge_ref = bf16[512,512]{1,0:T(8,128)(2,1)S(1)} collective-permute-done((bf16[512,512]{1,0:T(8,128)(2,1)S(1)}, bf16[512,512]{1,0:T(8,128)(2,1)S(1)}, u32[]{:S(2)}, u32[]{:S(2)}) %collective-permute-start.11) | collective-permute-done | bytes 524320 | tf_op jit(solution)/shard_map/ppermute | solution.py:433
  33.8 0.6 collective-permute-start.12
  34.4 1.3 %collective-permute-start.8 = (bf16[512,512]{1,0:T(8,128)(2,1)S(1)}, bf16[512,512]{1,0:T(8,128)(2,1)S(1)}, u32[]{:S(2)}, u32[]{:S(2)}) collective-permute-start(bf16[512,512]{1,0:T(8,128)(2,1)S(1)} %collective-permute-done.7.inner_ref), channel_id=1, source_target_pairs={{2,0},{3,1},{4,6},{5,7},{10,8},{11,9},{12,14},{13,15},{18,16},{19,... | collective-permute-start | bytes 1572872 | tf_op jit(solution)/shard_map/ppermute | solution.py:433
  35.7 0.0 collective-permute-done.3.refs_3_
  35.7 3.8 %collective-permute-start.4 = (bf16[512,512]{1,0:T(8,128)(2,1)S(1)}, bf16[512,512]{1,0:T(8,128)(2,1)S(1)}, u32[]{:S(2)}, u32[]{:S(2)}) collective-permute-start(bf16[512,512]{1,0:T(8,128)(2,1)S(1)} %collective-permute-done.3.refs_3_), channel_id=1, source_target_pairs={{0,6},{1,7},{6,0},{7,1},{8,14},{9,15},{14,8},{15,9},{16,22},{17,23... | collective-permute-start | bytes 1572872 | tf_op jit(solution)/shard_map/ppermute | solution.py:433
  39.5 0.7 collective-permute-start.5
  40.2 0.0 collective-permute-done.14.refs_2_
  40.2 1.6 %collective-permute-start.15 = (bf16[512,512]{1,0:T(8,128)(2,1)S(1)}, bf16[512,512]{1,0:T(8,128)(2,1)S(1)}, u32[]{:S(2)}, u32[]{:S(2)}) collective-permute-start(bf16[512,512]{1,0:T(8,128)(2,1)S(1)} %collective-permute-done.14.refs_2_), channel_id=1, source_target_pairs={{0,16},{1,17},{2,18},{3,19},{4,20},{5,21},{6,22},{7,23},{8,24},{9,... | collective-permute-start | bytes 1572872 | tf_op jit(solution)/shard_map/ppermute | solution.py:433
  41.8 4.8 %attend.6 = (f32[5,4,144,128]{3,2,1,0:T(8,128)S(1)}, f32[5,8,512]{2,1,0:T(8,128)S(1)}, f32[5,4,144,128]{3,2,1,0:T(8,128)S(1)}, f32[5,8,512]{2,1,0:T(8,128)S(1)}) custom-call(s32[640]{0:T(1024)S(1)} %get-tuple-element.28.refs_0_, bf16[512,512]{1,0:T(8,128)(2,1)S(1)} %pick.5.refs_1_, ...), custom_call_target="tpu_custom_call", output_to_operand_aliasing={{0}: (7, {}), {1}: (8, {}), {2}: (9, {}), {3}: (10, {})} | custom-call | flops 6000000000 | bytes 8388608 | tf_op jit(solution)/shard_map/attend/pallas_call | solution.py:340
  46.6 12.3 %collective-permute-done.8.edge_ref = bf16[512,512]{1,0:T(8,128)(2,1)S(1)} collective-permute-done((bf16[512,512]{1,0:T(8,128)(2,1)S(1)}, bf16[512,512]{1,0:T(8,128)(2,1)S(1)}, u32[]{:S(2)}, u32[]{:S(2)}) %collective-permute-start.8) | collective-permute-done | bytes 524320 | tf_op jit(solution)/shard_map/ppermute | solution.py:433
  59.0 1.6 %collective-permute-start.10 = (bf16[512,512]{1,0:T(8,128)(2,1)S(1)}, bf16[512,512]{1,0:T(8,128)(2,1)S(1)}, u32[]{:S(2)}, u32[]{:S(2)}) collective-permute-start(bf16[512,512]{1,0:T(8,128)(2,1)S(1)} %pick.4.refs_1_), channel_id=1, source_target_pairs={{0,8},{1,9},{2,10},{3,11},{4,12},{5,13},{6,14},{7,15},{8,0},{9,1},... | collective-permute-start | bytes 1572872 | tf_op jit(solution)/shard_map/ppermute | solution.py:433
  60.5 0.0 collective-permute-done.12.refs_2_
  60.5 1.5 %collective-permute-start.13 = (bf16[512,512]{1,0:T(8,128)(2,1)S(1)}, bf16[512,512]{1,0:T(8,128)(2,1)S(1)}, u32[]{:S(2)}, u32[]{:S(2)}) collective-permute-start(bf16[512,512]{1,0:T(8,128)(2,1)S(1)} %collective-permute-done.12.refs_2_), channel_id=1, source_target_pairs={{0,16},{1,17},{2,18},{3,19},{4,20},{5,21},{6,22},{7,23},{8,24},{9,... | collective-permute-start | bytes 1572872 | tf_op jit(solution)/shard_map/ppermute | solution.py:433
  62.0 0.0 collective-permute-done.4.edge_ref
  62.0 0.0 collective-permute-done.5.inner_ref
  62.0 0.2 pick.3.refs_1_
  62.3 0.0 collective-permute-done.15.refs_3_
  62.3 4.3 %attend.7 = (f32[5,4,144,128]{3,2,1,0:T(8,128)S(1)}, f32[5,8,512]{2,1,0:T(8,128)S(1)}, f32[5,4,144,128]{3,2,1,0:T(8,128)S(1)}, f32[5,8,512]{2,1,0:T(8,128)S(1)}) custom-call(s32[640]{0:T(1024)S(1)} %get-tuple-element.28.refs_0_, bf16[512,512]{1,0:T(8,128)(2,1)S(1)} %pick.4.refs_1_, ...), custom_call_target="tpu_custom_call", output_to_operand_aliasing={{0}: (7, {}), {1}: (8, {}), {2}: (9, {}), {3}: (10, {})} | custom-call | flops 6000000000 | bytes 8388608 | tf_op jit(solution)/shard_map/attend/pallas_call | solution.py:340
  66.6 4.4 %collective-permute-done.13.refs_2_ = bf16[512,512]{1,0:T(8,128)(2,1)S(1)} collective-permute-done((bf16[512,512]{1,0:T(8,128)(2,1)S(1)}, bf16[512,512]{1,0:T(8,128)(2,1)S(1)}, u32[]{:S(2)}, u32[]{:S(2)}) %collective-permute-start.13) | collective-permute-done | bytes 524320 | tf_op jit(solution)/shard_map/ppermute | solution.py:433
  71.0 0.0 collective-permute-done.10.refs_1_
  71.0 2.8 %attend.8 = (f32[5,4,144,128]{3,2,1,0:T(8,128)S(1)}, f32[5,8,512]{2,1,0:T(8,128)S(1)}, f32[5,4,144,128]{3,2,1,0:T(8,128)S(1)}, f32[5,8,512]{2,1,0:T(8,128)S(1)}) custom-call(s32[640]{0:T(1024)S(1)} %get-tuple-element.28.refs_0_, ...), custom_call_target="tpu_custom_call", output_to_operand_aliasing={{0}: (6, {}), {1}: (7, {}), {2}: (8, {}), {3}: (9, {})} | custom-call | flops 4000000000 | bytes 8388608 | tf_op jit(solution)/shard_map/attend/pallas_call | solution.py:340
  73.8 0.0 copy-start.1
  73.8 0.0 copy-start.2
  73.8 0.0 copy-start.3
  73.8 0.0 copy-start.5
  73.9 2.7 %attend.9 = (f32[5,4,144,128]{3,2,1,0:T(8,128)S(1)}, f32[5,8,512]{2,1,0:T(8,128)S(1)}, bf16[4,4,128,128]{3,2,1,0:T(8,128)(2,1)S(1)}, f32[4,8,512]{2,1,0:T(8,128)S(1)}) custom-call(s32[640]{0:T(1024)S(1)} %get-tuple-element.28.refs_0_, bf16[512,512]{1,0:T(8,128)(2,1)S(1)} %pick.3.refs_1_, ...), custom_call_target="tpu_custom_call", output_to_operand_aliasing={{0}: (5, {}), {1}: (6, {})} | custom-call | flops 2000000000 | bytes 8388608 | tf_op jit(solution)/shard_map/attend/pallas_call | solution.py:340
  76.6 0.1 collective-permute-start.16
  76.7 0.5 collective-permute-start.17
  77.2 1.5 %collective-permute-done.17.stat_ref = f32[4,8,512]{2,1,0:T(8,128)S(1)} collective-permute-done((f32[4,8,512]{2,1,0:T(8,128)S(1)}, f32[4,8,512]{2,1,0:T(8,128)S(1)}, u32[]{:S(2)}, u32[]{:S(2)}) %collective-permute-start.17) | collective-permute-done | bytes 65568 | tf_op jit(solution)/shard_map/ppermute | solution.py:433
  78.7 0.0 collective-permute-done.16.half_ref
  78.7 0.0 copy-done.1
  78.7 0.0 copy-done.2
  78.7 0.0 copy-done.3
  78.7 0.0 copy-done.5
  78.7 5.2 %finish.1 = bf16[512,512]{1,0:T(8,128)(2,1)} custom-call(f32[5,4,144,128]{3,2,1,0:T(8,128)S(1)} %get-tuple-element.47.acc_ref, f32[5,8,512]{2,1,0:T(8,128)S(1)} %get-tuple-element.48.top_ref, bf16[4,4,128,128]{3,2,1,0:T(8,128)(2,1)S(1)} %collective-permute-done.16.half_ref, f32[4,8,512]{2,1,0:T(8,128)S(1)} %collective-permute-done.17.stat_ref, ...), custom_call_target="tpu_custom_call" | custom-call | flops 3489660928 | bytes 12582912 | tf_op jit(solution)/shard_map/finish/pallas_call | solution.py:408
  (2 shorter events, 0.1 us)
Async XLA Ops:
  0.0 24.0 %copy-start = (bf16[512,512]{1,0:T(8,128)(2,1)S(1)}, bf16[512,512]{1,0:T(8,128)(2,1)}, u32[]{:S(2)}) copy-start(bf16[512,512]{1,0:T(8,128)(2,1)} %x_ref.1) | copy-start | bytes 1572868
  0.0 24.0 %copy-start.4 = (bf16[512,512]{1,0:T(8,128)(2,1)S(1)}, bf16[512,512]{1,0:T(8,128)(2,1)}, u32[]{:S(2)}) copy-start(bf16[512,512]{1,0:T(8,128)(2,1)} %refs_2_.3) | copy-start | bytes 1572868
  0.0 15.3 %collective-permute-start.6 = (bf16[512,512]{1,0:T(8,128)(2,1)}, bf16[512,512]{1,0:T(8,128)(2,1)S(1)}, u32[]{:S(2)}, u32[]{:S(2)}) collective-permute-start(bf16[512,512]{1,0:T(8,128)(2,1)} %x_ref.1), channel_id=1, source_target_pairs={{0,2},{1,3},{2,0},{3,1},{4,6},{5,7},{6,4},{7,5},{8,10},{9,11},{10,... | collective-permute-start | bytes 1572872 | tf_op jit(solution)/shard_map/ppermute | solution.py:433
  3.1 14.6 %collective-permute-start.9 = (bf16[512,512]{1,0:T(8,128)(2,1)}, bf16[512,512]{1,0:T(8,128)(2,1)S(1)}, u32[]{:S(2)}, u32[]{:S(2)}) collective-permute-start(bf16[512,512]{1,0:T(8,128)(2,1)} %x_ref.1), channel_id=1, source_target_pairs={{2,4},{3,5},{4,2},{5,3},{10,12},{11,13},{12,10},{13,11},{18,20},{1... | collective-permute-start | bytes 1572872 | tf_op jit(solution)/shard_map/ppermute | solution.py:433
  3.7 15.2 %collective-permute-start.2 = (bf16[512,512]{1,0:T(8,128)(2,1)}, bf16[512,512]{1,0:T(8,128)(2,1)S(1)}, u32[]{:S(2)}, u32[]{:S(2)}) collective-permute-start(bf16[512,512]{1,0:T(8,128)(2,1)} %x_ref.1), channel_id=1, source_target_pairs={{0,8},{1,9},{2,10},{3,11},{4,12},{5,13},{6,14},{7,15},{8,0},{9,1},... | collective-permute-start | bytes 1572872 | tf_op jit(solution)/shard_map/ppermute | solution.py:433
  5.3 15.2 %collective-permute-start.1 = (bf16[512,512]{1,0:T(8,128)(2,1)}, bf16[512,512]{1,0:T(8,128)(2,1)S(1)}, u32[]{:S(2)}, u32[]{:S(2)}) collective-permute-start(bf16[512,512]{1,0:T(8,128)(2,1)} %x_ref.1), channel_id=1, source_target_pairs={{0,1},{1,0},{2,3},{3,2},{4,5},{5,4},{6,7},{7,6},{8,9},{9,8},{10,11... | collective-permute-start | bytes 1572872 | tf_op jit(solution)/shard_map/ppermute | solution.py:433
  5.3 10.6 %collective-permute-start = (s32[4,32]{1,0:T(4,128)}, s32[4,32]{1,0:T(4,128)S(1)}, u32[]{:S(2)}, u32[]{:S(2)}) collective-permute-start(s32[4,32]{1,0:T(4,128)} %refs_2_.2), channel_id=1, source_target_pairs={{0,1},{1,0},{2,3},{3,2},{4,5},{5,4},{6,7},{7,6},{8,9},{9,8},{10,11... | collective-permute-start | bytes 1544 | tf_op jit(solution)/shard_map/ppermute | solution.py:433
  15.3 13.3 %collective-permute-start.7 = (bf16[512,512]{1,0:T(8,128)(2,1)S(1)}, bf16[512,512]{1,0:T(8,128)(2,1)S(1)}, u32[]{:S(2)}, u32[]{:S(2)}) collective-permute-start(bf16[512,512]{1,0:T(8,128)(2,1)S(1)} %collective-permute-done.6.refs_2_), channel_id=1, source_target_pairs={{2,4},{3,5},{4,2},{5,3},{10,12},{11,13},{12,10},{13,11},{18,20},{1... | collective-permute-start | bytes 1572872 | tf_op jit(solution)/shard_map/ppermute | solution.py:433
  16.0 24.2 %collective-permute-start.14 = (bf16[512,512]{1,0:T(8,128)(2,1)S(1)}, bf16[512,512]{1,0:T(8,128)(2,1)S(1)}, u32[]{:S(2)}, u32[]{:S(2)}) collective-permute-start(bf16[512,512]{1,0:T(8,128)(2,1)S(1)} %collective-permute-done.6.refs_2_), channel_id=1, source_target_pairs={{0,8},{1,9},{2,10},{3,11},{4,12},{5,13},{6,14},{7,15},{8,0},{9,1},... | collective-permute-start | bytes 1572872 | tf_op jit(solution)/shard_map/ppermute | solution.py:433
  17.6 16.1 %collective-permute-start.11 = (bf16[512,512]{1,0:T(8,128)(2,1)S(1)}, bf16[512,512]{1,0:T(8,128)(2,1)S(1)}, u32[]{:S(2)}, u32[]{:S(2)}) collective-permute-start(bf16[512,512]{1,0:T(8,128)(2,1)S(1)} %collective-permute-done.9.inner_ref), channel_id=1, source_target_pairs={{2,0},{3,1},{4,6},{5,7},{10,8},{11,9},{12,14},{13,15},{18,16},{19,... | collective-permute-start | bytes 1572872 | tf_op jit(solution)/shard_map/ppermute | solution.py:433
  18.9 16.8 %collective-permute-start.3 = (bf16[512,512]{1,0:T(8,128)(2,1)S(1)}, bf16[512,512]{1,0:T(8,128)(2,1)S(1)}, u32[]{:S(2)}, u32[]{:S(2)}) collective-permute-start(bf16[512,512]{1,0:T(8,128)(2,1)S(1)} %collective-permute-done.2.refs_3_), channel_id=1, source_target_pairs={{0,16},{1,17},{2,18},{3,19},{4,20},{5,21},{6,22},{7,23},{8,24},{9,... | collective-permute-start | bytes 1572872 | tf_op jit(solution)/shard_map/ppermute | solution.py:433
  33.8 26.7 %collective-permute-start.12 = (bf16[512,512]{1,0:T(8,128)(2,1)S(1)}, bf16[512,512]{1,0:T(8,128)(2,1)S(1)}, u32[]{:S(2)}, u32[]{:S(2)}) collective-permute-start(bf16[512,512]{1,0:T(8,128)(2,1)S(1)} %pick.5.refs_1_), channel_id=1, source_target_pairs={{0,8},{1,9},{2,10},{3,11},{4,12},{5,13},{6,14},{7,15},{8,0},{9,1},... | collective-permute-start | bytes 1572872 | tf_op jit(solution)/shard_map/ppermute | solution.py:433
  34.4 24.5 %collective-permute-start.8 = (bf16[512,512]{1,0:T(8,128)(2,1)S(1)}, bf16[512,512]{1,0:T(8,128)(2,1)S(1)}, u32[]{:S(2)}, u32[]{:S(2)}) collective-permute-start(bf16[512,512]{1,0:T(8,128)(2,1)S(1)} %collective-permute-done.7.inner_ref), channel_id=1, source_target_pairs={{2,0},{3,1},{4,6},{5,7},{10,8},{11,9},{12,14},{13,15},{18,16},{19,... | collective-permute-start | bytes 1572872 | tf_op jit(solution)/shard_map/ppermute | solution.py:433
  35.7 26.3 %collective-permute-start.4 = (bf16[512,512]{1,0:T(8,128)(2,1)S(1)}, bf16[512,512]{1,0:T(8,128)(2,1)S(1)}, u32[]{:S(2)}, u32[]{:S(2)}) collective-permute-start(bf16[512,512]{1,0:T(8,128)(2,1)S(1)} %collective-permute-done.3.refs_3_), channel_id=1, source_target_pairs={{0,6},{1,7},{6,0},{7,1},{8,14},{9,15},{14,8},{15,9},{16,22},{17,23... | collective-permute-start | bytes 1572872 | tf_op jit(solution)/shard_map/ppermute | solution.py:433
  39.5 22.5 %collective-permute-start.5 = (bf16[512,512]{1,0:T(8,128)(2,1)S(1)}, bf16[512,512]{1,0:T(8,128)(2,1)S(1)}, u32[]{:S(2)}, u32[]{:S(2)}) collective-permute-start(bf16[512,512]{1,0:T(8,128)(2,1)S(1)} %collective-permute-done.3.refs_3_), channel_id=1, source_target_pairs={{2,4},{3,5},{4,2},{5,3},{10,12},{11,13},{12,10},{13,11},{18,20},{1... | collective-permute-start | bytes 1572872 | tf_op jit(solution)/shard_map/ppermute | solution.py:433
  40.2 22.1 %collective-permute-start.15 = (bf16[512,512]{1,0:T(8,128)(2,1)S(1)}, bf16[512,512]{1,0:T(8,128)(2,1)S(1)}, u32[]{:S(2)}, u32[]{:S(2)}) collective-permute-start(bf16[512,512]{1,0:T(8,128)(2,1)S(1)} %collective-permute-done.14.refs_2_), channel_id=1, source_target_pairs={{0,16},{1,17},{2,18},{3,19},{4,20},{5,21},{6,22},{7,23},{8,24},{9,... | collective-permute-start | bytes 1572872 | tf_op jit(solution)/shard_map/ppermute | solution.py:433
  59.0 12.0 %collective-permute-start.10 = (bf16[512,512]{1,0:T(8,128)(2,1)S(1)}, bf16[512,512]{1,0:T(8,128)(2,1)S(1)}, u32[]{:S(2)}, u32[]{:S(2)}) collective-permute-start(bf16[512,512]{1,0:T(8,128)(2,1)S(1)} %pick.4.refs_1_), channel_id=1, source_target_pairs={{0,8},{1,9},{2,10},{3,11},{4,12},{5,13},{6,14},{7,15},{8,0},{9,1},... | collective-permute-start | bytes 1572872 | tf_op jit(solution)/shard_map/ppermute | solution.py:433
  60.5 10.5 %collective-permute-start.13 = (bf16[512,512]{1,0:T(8,128)(2,1)S(1)}, bf16[512,512]{1,0:T(8,128)(2,1)S(1)}, u32[]{:S(2)}, u32[]{:S(2)}) collective-permute-start(bf16[512,512]{1,0:T(8,128)(2,1)S(1)} %collective-permute-done.12.refs_2_), channel_id=1, source_target_pairs={{0,16},{1,17},{2,18},{3,19},{4,20},{5,21},{6,22},{7,23},{8,24},{9,... | collective-permute-start | bytes 1572872 | tf_op jit(solution)/shard_map/ppermute | solution.py:433
  73.8 4.9 %copy-start.1 = (bf16[512,2048]{1,0:T(8,128)(2,1)S(1)}, bf16[512,2048]{1,0:T(8,128)(2,1)}, u32[]{:S(2)}) copy-start(bf16[512,2048]{1,0:T(8,128)(2,1)} %wg_ref.1) | copy-start | bytes 6291460
  73.8 4.9 %copy-start.2 = (bf16[512,2048]{1,0:T(8,128)(2,1)S(1)}, bf16[512,2048]{1,0:T(8,128)(2,1)}, u32[]{:S(2)}) copy-start(bf16[512,2048]{1,0:T(8,128)(2,1)} %wu_ref.1) | copy-start | bytes 6291460
  73.8 4.9 %copy-start.3 = (bf16[2048,512]{1,0:T(8,128)(2,1)S(1)}, bf16[2048,512]{1,0:T(8,128)(2,1)}, u32[]{:S(2)}) copy-start(bf16[2048,512]{1,0:T(8,128)(2,1)} %wd_ref.1) | copy-start | bytes 6291460
  73.8 4.9 %copy-start.5 = (bf16[512,512]{1,0:T(8,128)(2,1)S(1)}, bf16[512,512]{1,0:T(8,128)(2,1)}, u32[]{:S(2)}) copy-start(bf16[512,512]{1,0:T(8,128)(2,1)} %wo_ref.1) | copy-start | bytes 1572868
  76.6 2.1 %collective-permute-start.16 = (bf16[4,4,128,128]{3,2,1,0:T(8,128)(2,1)S(1)}, bf16[4,4,128,128]{3,2,1,0:T(8,128)(2,1)S(1)}, u32[]{:S(2)}, u32[]{:S(2)}) collective-permute-start(bf16[4,4,128,128]{3,2,1,0:T(8,128)(2,1)S(1)} %get-tuple-element.49), channel_id=1, source_target_pairs={{0,1},{1,0},{2,3},{3,2},{4,5},{5,4},{6,7},{7,6},{8,9},{9,8},{10,11... | collective-permute-start | bytes 1572872 | tf_op jit(solution)/shard_map/ppermute | solution.py:433
  76.7 2.0 %collective-permute-start.17 = (f32[4,8,512]{2,1,0:T(8,128)S(1)}, f32[4,8,512]{2,1,0:T(8,128)S(1)}, u32[]{:S(2)}, u32[]{:S(2)}) collective-permute-start(f32[4,8,512]{2,1,0:T(8,128)S(1)} %get-tuple-element.50), channel_id=1, source_target_pairs={{0,1},{1,0},{2,3},{3,2},{4,5},{5,4},{6,7},{7,6},{8,9},{9,8},{10,11... | collective-permute-start | bytes 196616 | tf_op jit(solution)/shard_map/ppermute | solution.py:433
